TPU v7x, 512 devices: a whole 4x4x16 slice. The times are simulated.
512 devices in a mesh: slot: 16 (over z_lo, x), row: 32 (over y, z_hi, core).
Axes of the slice: x: 4, y: 4, z: 16 (z_hi: 4, z_lo: 4; z = z_hi * 4 + z_lo), core: 2. Of those that a mesh axis runs over, the one named last changes fastest.
Arguments:
- drift: bfloat16 [2048, 2048], P(('slot', 'row')), may hold values from -1 to 1, as said below
- ctrl_blocks: bfloat16 [16, 128, 128], replicated, may hold values from -0.125 to 0.125
- blk_pos: int32 [16, 2], replicated, may hold values from 0 to 15
- amps: float32 [16, 16], P('slot'), may hold values from -4 to 4
- init_states: float32 [2, 512, 2048], P(None, 'row'), may hold values from -6 to 6
- targets: float32 [2, 512, 2048], P(None, 'row'), may hold values from -50 to 50
Outputs:
- states: float32 [16, 2, 512, 2048], P('slot', None, 'row')
- grads: float32 [16, 16], P('slot')
Inputs may be any that keep to these rules, and one draw needn't show every extreme that they name: drift is symmetric.
All inputs are finite; a program needn't handle non-finite values.
Results may differ from a plain program's by a relative error of at most 0.038.
Values may be sent and summed in bfloat16 or wider, within the bound.
No kernel may reach another device: no remote copies, remote signals or barrier semaphores. Data moves between devices by JAX's collectives and lax.ppermute only.
A program may use at most 64 MiB of HBM per device.

v0:
```python
import jax
import jax.numpy as jnp
from jax import lax
from jax.sharding import PartitionSpec as P

TAYLOR = 4


def passed_along(value, axis, steps):
    count = lax.axis_size(axis)
    initial, last = (max(0, -steps), min(count, count - steps))
    return lax.ppermute(value, axis, [(source, source + steps) for source in range(initial, last)])


def apply_hamiltonian(
    rounded, drift_full, ctrl_blocks, row_pick, col_pick, row_hot, col_hot, amps_row
):
    halves, columns, extent = rounded.shape
    block_size = ctrl_blocks.shape[1]
    flat_rows = rounded.reshape(halves * columns, extent)
    drift_part = jnp.dot(flat_rows, drift_full, preferred_element_type=jnp.float32)
    tile_rows = flat_rows.reshape(halves * columns, extent // block_size, block_size)
    from_col = jnp.take(tile_rows, col_pick, axis=1)
    from_row = jnp.take(tile_rows, row_pick, axis=1)
    upper_part = (
        jnp.einsum("mkb,kab->mka", from_col, ctrl_blocks, preferred_element_type=jnp.float32)
        * amps_row[None, :, None]
    )
    lower_part = (
        jnp.einsum("mka,kab->mkb", from_row, ctrl_blocks, preferred_element_type=jnp.float32)
        * amps_row[None, :, None]
    )
    placed = jnp.einsum("mka,kn->mna", upper_part, row_hot, precision=lax.Precision.HIGHEST)
    placed = placed + jnp.einsum(
        "mkb,kn->mnb", lower_part, col_hot, precision=lax.Precision.HIGHEST
    )
    summed = drift_part + placed.reshape(halves * columns, extent)
    return summed.reshape(halves, columns, extent)


def propagate(state, forward, apply_fn):
    summed = state
    series_term = state
    for degree in range(1, TAYLOR + 1):
        applied = apply_fn(series_term.astype(jnp.bfloat16))
        if forward:
            turned = jnp.stack([applied[1], -applied[0]])
        else:
            turned = jnp.stack([-applied[1], applied[0]])
        series_term = turned * (1.0 / degree)
        summed = summed + series_term
    return summed


def control_grads(state, adjoint, ctrl_blocks, row_pick, col_pick, scale):
    halves, columns, extent = state.shape
    block_size = ctrl_blocks.shape[1]
    shape_tiles = (halves * columns, extent // block_size, block_size)
    source = jnp.stack([state[1].astype(jnp.bfloat16), -state[0].astype(jnp.bfloat16)]).reshape(
        shape_tiles
    )
    weights = adjoint.astype(jnp.bfloat16).reshape(shape_tiles)
    upper_part = jnp.einsum(
        "mkb,kab->mka",
        jnp.take(source, col_pick, axis=1),
        ctrl_blocks,
        preferred_element_type=jnp.float32,
    )
    lower_part = jnp.einsum(
        "mka,kab->mkb",
        jnp.take(source, row_pick, axis=1),
        ctrl_blocks,
        preferred_element_type=jnp.float32,
    )
    inner_sum = jnp.sum(
        jnp.take(weights, row_pick, axis=1).astype(jnp.float32) * upper_part, axis=(0, 2)
    )
    inner_sum = inner_sum + jnp.sum(
        jnp.take(weights, col_pick, axis=1).astype(jnp.float32) * lower_part, axis=(0, 2)
    )
    return inner_sum * scale


def blank(values):
    return jnp.zeros_like(values)


def shards(drift, ctrl_blocks, blk_pos, amps, init_states, targets):
    drift_full = lax.all_gather(drift, ("slot", "row"), axis=0, tiled=True)
    block_count = drift_full.shape[0] // ctrl_blocks.shape[1]
    row_pick = blk_pos[:, 0]
    col_pick = blk_pos[:, 1]
    positions = lax.broadcasted_iota(jnp.int32, (ctrl_blocks.shape[0], block_count), 1)
    row_hot = (positions == row_pick[:, None]).astype(jnp.float32)
    col_hot = (positions == col_pick[:, None]).astype(jnp.float32)
    amps_row = amps[0]

    def apply_fn(rounded):
        return apply_hamiltonian(
            rounded, drift_full, ctrl_blocks, row_pick, col_pick, row_hot, col_hot, amps_row
        )

    def forward_map(values):
        return propagate(values, True, apply_fn)

    def adjoint_map(values):
        return propagate(values, False, apply_fn)

    slot_index = lax.axis_index("slot")
    slot_count = lax.axis_size("slot")
    last_slot = slot_count - 1
    columns = init_states.shape[1]
    extent = init_states.shape[2]
    piece_count = 1
    width = columns // piece_count

    def split_cols(values):
        return values.reshape(2, piece_count, width, extent).transpose(1, 0, 2, 3)

    def join_cols(pieces):
        return pieces.transpose(1, 0, 2, 3).reshape(2, columns, extent)

    init_pieces = split_cols(init_states)
    target_pieces = split_cols(targets)
    tick_count = slot_count + piece_count - 1
    empty_all = jnp.zeros_like(init_pieces)
    empty_one = jnp.zeros_like(init_pieces[0])

    def forward_update(step, stored, arrived):
        order = step - slot_index
        active = (order >= 0) & (order < piece_count)
        place = jnp.clip(order, 0, piece_count - 1)
        start_piece = lax.dynamic_index_in_dim(init_pieces, place, 0, keepdims=False)
        source = jnp.where(slot_index == 0, start_piece, arrived)
        result = lax.cond(active, forward_map, blank, source)
        updated = lax.dynamic_update_index_in_dim(stored, result, place, 0)
        stored = jnp.where(active, updated, stored)
        return (stored, result)

    def adjoint_update(step, stored, returned):
        order = step - (last_slot - slot_index)
        active = (order >= 0) & (order < piece_count)
        place = jnp.clip(order, 0, piece_count - 1)
        target_piece = lax.dynamic_index_in_dim(target_pieces, place, 0, keepdims=False)
        own = jnp.where(slot_index == last_slot, target_piece, returned)
        updated = lax.dynamic_update_index_in_dim(stored, own, place, 0)
        stored = jnp.where(active, updated, stored)
        outgoing = lax.cond(active & (slot_index > 0), adjoint_map, blank, own)
        return (stored, outgoing)

    def joint_tick(step, carry):
        fwd_stored, fwd_out, adj_stored, adj_out = carry
        arrived = passed_along(fwd_out.astype(jnp.bfloat16), "slot", 1).astype(fwd_out.dtype)
        returned = passed_along(adj_out.astype(jnp.bfloat16), "slot", -1).astype(adj_out.dtype)
        fwd_stored, fwd_out = forward_update(step, fwd_stored, arrived)
        adj_stored, adj_out = adjoint_update(step, adj_stored, returned)
        return (fwd_stored, fwd_out, adj_stored, adj_out)

    fwd_stored, _, adj_stored, _ = lax.fori_loop(
        0, tick_count, joint_tick, (empty_all, empty_one, empty_all, empty_one)
    )
    fwd_state = join_cols(fwd_stored)
    adj_mine = join_cols(adj_stored)
    scale = 1.0 / (columns * lax.axis_size("row"))
    partial_grads = control_grads(fwd_state, adj_mine, ctrl_blocks, row_pick, col_pick, scale)
    grads = lax.psum(partial_grads[None, :], "row")
    return (fwd_state[None], grads)


def solution(mesh):
    in_specs = (
        P(("slot", "row"), None),
        P(),
        P(),
        P("slot", None),
        P(None, "row", None),
        P(None, "row", None),
    )
    out_specs = (P("slot", None, "row", None), P("slot", None))
    return jax.shard_map(shards, mesh=mesh, in_specs=in_specs, out_specs=out_specs, check_vma=False)
```

profile of v0, /device:TPU:1, one launch (start us, length us, event | category | flops | bytes accessed | tf_op | source)
XLA Modules:
  0.0 1640.7 jit_solution(1172429229301434716)
XLA Ops:
  11.2 823.3 %all-gather.3.cloned.1.call-done = bf16[512,4,2048]{2,1,0:T(4,128)(2,1)} async-done(((bf16[1,4,2048]{2,1,0:T(4,128)(2,1)}), bf16[512,4,2048]{2,1,0:T(4,128)(2,1)}) %all-gather.3.cloned.1.call-update) | async-done | bytes 8388624 | tf_op jit(solution)/shard_map/all_gather | solution.py:89
  834.6 12.5 reshape.382
  847.9 668.3 %while.23 = (s32[]{:T(128)}, f32[1,2,16,2048]{3,2,1,0:T(8,128)S(1)}, f32[2,16,2048]{2,1,0:T(8,128)}, bf16[1,2,16,2048]{3,2,1,0:T(8,128)(2,1)S(1)}, bf16[2,16,204...) while((s32[]{:T(128)}, ...), condition=%wide.region_5.7_spmd.clone.clone.clone, body=%wide.region_0.6_spmd.clone.clone.clone.sunk | while | flops 2623804928 | bytes 120887232 | solution.py:159
  856.9 33.8 %conditional.10 = (f32[2,16,2048]{2,1,0:T(8,128)}, f32[1,2,16,2048]{3,2,1,0:T(8,128)S(1)}) conditional(s32[]{:T(128)} %convert_element_type.215, () %tuple.104, (pred[]{:T(512)}, f32[1,2,16,2048]{3,2,1,0:T(8,128)S(1)}, f32[2,16,2048]{2,1,0:T(8,128)S(1)}, bf16[2048,2048]{1,0:T(8,128)(2,1)}, s32[16]{0:T(128)S(1)}, ...), branch_computations={%region_1.1_spmd, %region_2.3_spmd} | conditional | flops 1311639808 | bytes 59262640 | solution.py:135
  902.2 34.7 %collective-permute-start = (bf16[2,16,2048]{2,1,0:T(8,128)(2,1)S(1)}, bf16[2,16,2048]{2,1,0:T(8,128)(2,1)S(1)}, u32[]{:S(2)}, u32[]{:S(2)}) collective-permute-start(bf16[2,16,2048]{2,1,0:T(8,128)(2,1)S(1)} %convert_element_type.216), channel_id=1, source_target_pairs={{0,32},{32,64},{64,96},{96,128},{128,160},{160,192},{192,224},{224... | collective-permute-start | bytes 393224 | tf_op jit(solution)/shard_map/while/body/eval_jaxpr/ppermute | solution.py:12
  948.7 35.9 %collective-permute-done.1 = bf16[2,16,2048]{2,1,0:T(8,128)(2,1)S(1)} collective-permute-done((bf16[2,16,2048]{2,1,0:T(8,128)(2,1)}, bf16[2,16,2048]{2,1,0:T(8,128)(2,1)S(1)}, u32[]{:S(2)}, u32[]{:S(2)}) %collective-permute-start.1) | collective-permute-done | bytes 131104 | tf_op jit(solution)/shard_map/while/body/eval_jaxpr/ppermute | solution.py:12
  999.2 33.1 %collective-permute-start = (bf16[2,16,2048]{2,1,0:T(8,128)(2,1)S(1)}, bf16[2,16,2048]{2,1,0:T(8,128)(2,1)S(1)}, u32[]{:S(2)}, u32[]{:S(2)}) collective-permute-start(bf16[2,16,2048]{2,1,0:T(8,128)(2,1)S(1)} %convert_element_type.216), channel_id=1, source_target_pairs={{0,32},{32,64},{64,96},{96,128},{128,160},{160,192},{192,224},{224... | collective-permute-start | bytes 393224 | tf_op jit(solution)/shard_map/while/body/eval_jaxpr/ppermute | solution.py:12
  1046.5 35.5 %collective-permute-done.1 = bf16[2,16,2048]{2,1,0:T(8,128)(2,1)S(1)} collective-permute-done((bf16[2,16,2048]{2,1,0:T(8,128)(2,1)}, bf16[2,16,2048]{2,1,0:T(8,128)(2,1)S(1)}, u32[]{:S(2)}, u32[]{:S(2)}) %collective-permute-start.1) | collective-permute-done | bytes 131104 | tf_op jit(solution)/shard_map/while/body/eval_jaxpr/ppermute | solution.py:12
  1084.6 5.5 collective-permute-start
  1091.5 5.5 collective-permute-done.1
  1099.6 30.2 %collective-permute-start = (bf16[2,16,2048]{2,1,0:T(8,128)(2,1)S(1)}, bf16[2,16,2048]{2,1,0:T(8,128)(2,1)S(1)}, u32[]{:S(2)}, u32[]{:S(2)}) collective-permute-start(bf16[2,16,2048]{2,1,0:T(8,128)(2,1)S(1)} %convert_element_type.216), channel_id=1, source_target_pairs={{0,32},{32,64},{64,96},{96,128},{128,160},{160,192},{192,224},{224... | collective-permute-start | bytes 393224 | tf_op jit(solution)/shard_map/while/body/eval_jaxpr/ppermute | solution.py:12
  1138.3 7.5 collective-permute-start
  1147.1 30.3 %collective-permute-done.1 = bf16[2,16,2048]{2,1,0:T(8,128)(2,1)S(1)} collective-permute-done((bf16[2,16,2048]{2,1,0:T(8,128)(2,1)}, bf16[2,16,2048]{2,1,0:T(8,128)(2,1)S(1)}, u32[]{:S(2)}, u32[]{:S(2)}) %collective-permute-start.1) | collective-permute-done | bytes 131104 | tf_op jit(solution)/shard_map/while/body/eval_jaxpr/ppermute | solution.py:12
  1180.0 5.5 collective-permute-start
  1186.8 5.0 collective-permute-done.1
  1194.5 38.3 %collective-permute-start = (bf16[2,16,2048]{2,1,0:T(8,128)(2,1)S(1)}, bf16[2,16,2048]{2,1,0:T(8,128)(2,1)S(1)}, u32[]{:S(2)}, u32[]{:S(2)}) collective-permute-start(bf16[2,16,2048]{2,1,0:T(8,128)(2,1)S(1)} %convert_element_type.216), channel_id=1, source_target_pairs={{0,32},{32,64},{64,96},{96,128},{128,160},{160,192},{192,224},{224... | collective-permute-start | bytes 393224 | tf_op jit(solution)/shard_map/while/body/eval_jaxpr/ppermute | solution.py:12
  1241.3 36.7 %collective-permute-start = (bf16[2,16,2048]{2,1,0:T(8,128)(2,1)S(1)}, bf16[2,16,2048]{2,1,0:T(8,128)(2,1)S(1)}, u32[]{:S(2)}, u32[]{:S(2)}) collective-permute-start(bf16[2,16,2048]{2,1,0:T(8,128)(2,1)S(1)} %convert_element_type.216), channel_id=1, source_target_pairs={{0,32},{32,64},{64,96},{96,128},{128,160},{160,192},{192,224},{224... | collective-permute-start | bytes 393224 | tf_op jit(solution)/shard_map/while/body/eval_jaxpr/ppermute | solution.py:12
  1279.3 36.7 %collective-permute-done.1 = bf16[2,16,2048]{2,1,0:T(8,128)(2,1)S(1)} collective-permute-done((bf16[2,16,2048]{2,1,0:T(8,128)(2,1)}, bf16[2,16,2048]{2,1,0:T(8,128)(2,1)S(1)}, u32[]{:S(2)}, u32[]{:S(2)}) %collective-permute-start.1) | collective-permute-done | bytes 131104 | tf_op jit(solution)/shard_map/while/body/eval_jaxpr/ppermute | solution.py:12
  1318.6 35.5 %collective-permute-start = (bf16[2,16,2048]{2,1,0:T(8,128)(2,1)S(1)}, bf16[2,16,2048]{2,1,0:T(8,128)(2,1)S(1)}, u32[]{:S(2)}, u32[]{:S(2)}) collective-permute-start(bf16[2,16,2048]{2,1,0:T(8,128)(2,1)S(1)} %convert_element_type.216), channel_id=1, source_target_pairs={{0,32},{32,64},{64,96},{96,128},{128,160},{160,192},{192,224},{224... | collective-permute-start | bytes 393224 | tf_op jit(solution)/shard_map/while/body/eval_jaxpr/ppermute | solution.py:12
  1355.5 36.7 %collective-permute-done.1 = bf16[2,16,2048]{2,1,0:T(8,128)(2,1)S(1)} collective-permute-done((bf16[2,16,2048]{2,1,0:T(8,128)(2,1)}, bf16[2,16,2048]{2,1,0:T(8,128)(2,1)S(1)}, u32[]{:S(2)}, u32[]{:S(2)}) %collective-permute-start.1) | collective-permute-done | bytes 131104 | tf_op jit(solution)/shard_map/while/body/eval_jaxpr/ppermute | solution.py:12
  1394.8 37.6 %collective-permute-start = (bf16[2,16,2048]{2,1,0:T(8,128)(2,1)S(1)}, bf16[2,16,2048]{2,1,0:T(8,128)(2,1)S(1)}, u32[]{:S(2)}, u32[]{:S(2)}) collective-permute-start(bf16[2,16,2048]{2,1,0:T(8,128)(2,1)S(1)} %convert_element_type.216), channel_id=1, source_target_pairs={{0,32},{32,64},{64,96},{96,128},{128,160},{160,192},{192,224},{224... | collective-permute-start | bytes 393224 | tf_op jit(solution)/shard_map/while/body/eval_jaxpr/ppermute | solution.py:12
  1433.8 36.7 %collective-permute-done.1 = bf16[2,16,2048]{2,1,0:T(8,128)(2,1)S(1)} collective-permute-done((bf16[2,16,2048]{2,1,0:T(8,128)(2,1)}, bf16[2,16,2048]{2,1,0:T(8,128)(2,1)S(1)}, u32[]{:S(2)}, u32[]{:S(2)}) %collective-permute-start.1) | collective-permute-done | bytes 131104 | tf_op jit(solution)/shard_map/while/body/eval_jaxpr/ppermute | solution.py:12
  1473.1 35.5 %collective-permute-start = (bf16[2,16,2048]{2,1,0:T(8,128)(2,1)S(1)}, bf16[2,16,2048]{2,1,0:T(8,128)(2,1)S(1)}, u32[]{:S(2)}, u32[]{:S(2)}) collective-permute-start(bf16[2,16,2048]{2,1,0:T(8,128)(2,1)S(1)} %convert_element_type.216), channel_id=1, source_target_pairs={{0,32},{32,64},{64,96},{96,128},{128,160},{160,192},{192,224},{224... | collective-permute-start | bytes 393224 | tf_op jit(solution)/shard_map/while/body/eval_jaxpr/ppermute | solution.py:12
  1520.1 113.7 %psum.7 = f32[1,16]{1,0:T(1,128)} all-reduce(f32[1,16]{1,0:T(1,128)S(1)} %multiply_bitcast_fusion), channel_id=1, replica_groups=mesh['slot'=16,'row'=32] {'row'}, use_global_device_ids=true, to_apply=%region_8.10 | all-reduce | flops 16 | bytes 128 | tf_op jit(solution)/shard_map/psum | solution.py:166
  (289 shorter events, 174.7 us)
Async XLA Ops:
  7.2 827.4 %all-gather.3.cloned.1.call-start = ((), (), s32[]{:S(2)}) async-start(), calls=%async_computation | async-start | bytes 8404992 | tf_op jit(solution)/shard_map/all_gather | solution.py:89
  848.8 8.0 collective-permute-start
  892.4 7.3 collective-permute-start
  902.2 40.7 %collective-permute-start = (bf16[2,16,2048]{2,1,0:T(8,128)(2,1)S(1)}, bf16[2,16,2048]{2,1,0:T(8,128)(2,1)S(1)}, u32[]{:S(2)}, u32[]{:S(2)}) collective-permute-start(bf16[2,16,2048]{2,1,0:T(8,128)(2,1)S(1)} %convert_element_type.216), channel_id=1, source_target_pairs={{0,32},{32,64},{64,96},{96,128},{128,160},{160,192},{192,224},{224... | collective-permute-start | bytes 393224 | tf_op jit(solution)/shard_map/while/body/eval_jaxpr/ppermute | solution.py:12
  945.4 39.2 %collective-permute-start = (bf16[2,16,2048]{2,1,0:T(8,128)(2,1)S(1)}, bf16[2,16,2048]{2,1,0:T(8,128)(2,1)S(1)}, u32[]{:S(2)}, u32[]{:S(2)}) collective-permute-start(bf16[2,16,2048]{2,1,0:T(8,128)(2,1)S(1)} %convert_element_type.216), channel_id=1, source_target_pairs={{0,32},{32,64},{64,96},{96,128},{128,160},{160,192},{192,224},{224... | collective-permute-start | bytes 393224 | tf_op jit(solution)/shard_map/while/body/eval_jaxpr/ppermute | solution.py:12
  947.3 37.2 %collective-permute-start.1 = (bf16[2,16,2048]{2,1,0:T(8,128)(2,1)}, bf16[2,16,2048]{2,1,0:T(8,128)(2,1)S(1)}, u32[]{:S(2)}, u32[]{:S(2)}) collective-permute-start(bf16[2,16,2048]{2,1,0:T(8,128)(2,1)} %get-tuple-element.768), channel_id=1, source_target_pairs={{32,0},{64,32},{96,64},{128,96},{160,128},{192,160},{224,192},{256... | collective-permute-start | bytes 393224 | tf_op jit(solution)/shard_map/while/body/eval_jaxpr/ppermute | solution.py:12
  987.2 9.5 collective-permute-start
  999.2 39.1 %collective-permute-start = (bf16[2,16,2048]{2,1,0:T(8,128)(2,1)S(1)}, bf16[2,16,2048]{2,1,0:T(8,128)(2,1)S(1)}, u32[]{:S(2)}, u32[]{:S(2)}) collective-permute-start(bf16[2,16,2048]{2,1,0:T(8,128)(2,1)S(1)} %convert_element_type.216), channel_id=1, source_target_pairs={{0,32},{32,64},{64,96},{96,128},{128,160},{160,192},{192,224},{224... | collective-permute-start | bytes 393224 | tf_op jit(solution)/shard_map/while/body/eval_jaxpr/ppermute | solution.py:12
  1040.8 41.3 %collective-permute-start = (bf16[2,16,2048]{2,1,0:T(8,128)(2,1)S(1)}, bf16[2,16,2048]{2,1,0:T(8,128)(2,1)S(1)}, u32[]{:S(2)}, u32[]{:S(2)}) collective-permute-start(bf16[2,16,2048]{2,1,0:T(8,128)(2,1)S(1)} %convert_element_type.216), channel_id=1, source_target_pairs={{0,32},{32,64},{64,96},{96,128},{128,160},{160,192},{192,224},{224... | collective-permute-start | bytes 393224 | tf_op jit(solution)/shard_map/while/body/eval_jaxpr/ppermute | solution.py:12
  1045.2 36.9 %collective-permute-start.1 = (bf16[2,16,2048]{2,1,0:T(8,128)(2,1)}, bf16[2,16,2048]{2,1,0:T(8,128)(2,1)S(1)}, u32[]{:S(2)}, u32[]{:S(2)}) collective-permute-start(bf16[2,16,2048]{2,1,0:T(8,128)(2,1)} %get-tuple-element.768), channel_id=1, source_target_pairs={{32,0},{64,32},{96,64},{128,96},{160,128},{192,160},{224,192},{256... | collective-permute-start | bytes 393224 | tf_op jit(solution)/shard_map/while/body/eval_jaxpr/ppermute | solution.py:12
  1084.6 12.4 collective-permute-start
  1090.1 6.8 collective-permute-start.1
  1099.6 36.2 %collective-permute-start = (bf16[2,16,2048]{2,1,0:T(8,128)(2,1)S(1)}, bf16[2,16,2048]{2,1,0:T(8,128)(2,1)S(1)}, u32[]{:S(2)}, u32[]{:S(2)}) collective-permute-start(bf16[2,16,2048]{2,1,0:T(8,128)(2,1)S(1)} %convert_element_type.216), channel_id=1, source_target_pairs={{0,32},{32,64},{64,96},{96,128},{128,160},{160,192},{192,224},{224... | collective-permute-start | bytes 393224 | tf_op jit(solution)/shard_map/while/body/eval_jaxpr/ppermute | solution.py:12
  1138.3 39.2 %collective-permute-start = (bf16[2,16,2048]{2,1,0:T(8,128)(2,1)S(1)}, bf16[2,16,2048]{2,1,0:T(8,128)(2,1)S(1)}, u32[]{:S(2)}, u32[]{:S(2)}) collective-permute-start(bf16[2,16,2048]{2,1,0:T(8,128)(2,1)S(1)} %convert_element_type.216), channel_id=1, source_target_pairs={{0,32},{32,64},{64,96},{96,128},{128,160},{160,192},{192,224},{224... | collective-permute-start | bytes 393224 | tf_op jit(solution)/shard_map/while/body/eval_jaxpr/ppermute | solution.py:12
  1145.8 31.7 %collective-permute-start.1 = (bf16[2,16,2048]{2,1,0:T(8,128)(2,1)}, bf16[2,16,2048]{2,1,0:T(8,128)(2,1)S(1)}, u32[]{:S(2)}, u32[]{:S(2)}) collective-permute-start(bf16[2,16,2048]{2,1,0:T(8,128)(2,1)} %get-tuple-element.768), channel_id=1, source_target_pairs={{32,0},{64,32},{96,64},{128,96},{160,128},{192,160},{224,192},{256... | collective-permute-start | bytes 393224 | tf_op jit(solution)/shard_map/while/body/eval_jaxpr/ppermute | solution.py:12
  1180.0 11.9 collective-permute-start
  1194.5 44.3 %collective-permute-start = (bf16[2,16,2048]{2,1,0:T(8,128)(2,1)S(1)}, bf16[2,16,2048]{2,1,0:T(8,128)(2,1)S(1)}, u32[]{:S(2)}, u32[]{:S(2)}) collective-permute-start(bf16[2,16,2048]{2,1,0:T(8,128)(2,1)S(1)} %convert_element_type.216), channel_id=1, source_target_pairs={{0,32},{32,64},{64,96},{96,128},{128,160},{160,192},{192,224},{224... | collective-permute-start | bytes 393224 | tf_op jit(solution)/shard_map/while/body/eval_jaxpr/ppermute | solution.py:12
  1241.3 74.8 %collective-permute-start = (bf16[2,16,2048]{2,1,0:T(8,128)(2,1)S(1)}, bf16[2,16,2048]{2,1,0:T(8,128)(2,1)S(1)}, u32[]{:S(2)}, u32[]{:S(2)}) collective-permute-start(bf16[2,16,2048]{2,1,0:T(8,128)(2,1)S(1)} %convert_element_type.216), channel_id=1, source_target_pairs={{0,32},{32,64},{64,96},{96,128},{128,160},{160,192},{192,224},{224... | collective-permute-start | bytes 393224 | tf_op jit(solution)/shard_map/while/body/eval_jaxpr/ppermute | solution.py:12
  1278.0 38.1 %collective-permute-start.1 = (bf16[2,16,2048]{2,1,0:T(8,128)(2,1)}, bf16[2,16,2048]{2,1,0:T(8,128)(2,1)S(1)}, u32[]{:S(2)}, u32[]{:S(2)}) collective-permute-start(bf16[2,16,2048]{2,1,0:T(8,128)(2,1)} %get-tuple-element.768), channel_id=1, source_target_pairs={{32,0},{64,32},{96,64},{128,96},{160,128},{192,160},{224,192},{256... | collective-permute-start | bytes 393224 | tf_op jit(solution)/shard_map/while/body/eval_jaxpr/ppermute | solution.py:12
  1318.6 73.6 %collective-permute-start = (bf16[2,16,2048]{2,1,0:T(8,128)(2,1)S(1)}, bf16[2,16,2048]{2,1,0:T(8,128)(2,1)S(1)}, u32[]{:S(2)}, u32[]{:S(2)}) collective-permute-start(bf16[2,16,2048]{2,1,0:T(8,128)(2,1)S(1)} %convert_element_type.216), channel_id=1, source_target_pairs={{0,32},{32,64},{64,96},{96,128},{128,160},{160,192},{192,224},{224... | collective-permute-start | bytes 393224 | tf_op jit(solution)/shard_map/while/body/eval_jaxpr/ppermute | solution.py:12
  1354.2 38.1 %collective-permute-start.1 = (bf16[2,16,2048]{2,1,0:T(8,128)(2,1)}, bf16[2,16,2048]{2,1,0:T(8,128)(2,1)S(1)}, u32[]{:S(2)}, u32[]{:S(2)}) collective-permute-start(bf16[2,16,2048]{2,1,0:T(8,128)(2,1)} %get-tuple-element.768), channel_id=1, source_target_pairs={{32,0},{64,32},{96,64},{128,96},{160,128},{192,160},{224,192},{256... | collective-permute-start | bytes 393224 | tf_op jit(solution)/shard_map/while/body/eval_jaxpr/ppermute | solution.py:12
  1394.8 75.8 %collective-permute-start = (bf16[2,16,2048]{2,1,0:T(8,128)(2,1)S(1)}, bf16[2,16,2048]{2,1,0:T(8,128)(2,1)S(1)}, u32[]{:S(2)}, u32[]{:S(2)}) collective-permute-start(bf16[2,16,2048]{2,1,0:T(8,128)(2,1)S(1)} %convert_element_type.216), channel_id=1, source_target_pairs={{0,32},{32,64},{64,96},{96,128},{128,160},{160,192},{192,224},{224... | collective-permute-start | bytes 393224 | tf_op jit(solution)/shard_map/while/body/eval_jaxpr/ppermute | solution.py:12
  1432.4 38.1 %collective-permute-start.1 = (bf16[2,16,2048]{2,1,0:T(8,128)(2,1)}, bf16[2,16,2048]{2,1,0:T(8,128)(2,1)S(1)}, u32[]{:S(2)}, u32[]{:S(2)}) collective-permute-start(bf16[2,16,2048]{2,1,0:T(8,128)(2,1)} %get-tuple-element.768), channel_id=1, source_target_pairs={{32,0},{64,32},{96,64},{128,96},{160,128},{192,160},{224,192},{256... | collective-permute-start | bytes 393224 | tf_op jit(solution)/shard_map/while/body/eval_jaxpr/ppermute | solution.py:12
  1473.1 41.5 %collective-permute-start = (bf16[2,16,2048]{2,1,0:T(8,128)(2,1)S(1)}, bf16[2,16,2048]{2,1,0:T(8,128)(2,1)S(1)}, u32[]{:S(2)}, u32[]{:S(2)}) collective-permute-start(bf16[2,16,2048]{2,1,0:T(8,128)(2,1)S(1)} %convert_element_type.216), channel_id=1, source_target_pairs={{0,32},{32,64},{64,96},{96,128},{128,160},{160,192},{192,224},{224... | collective-permute-start | bytes 393224 | tf_op jit(solution)/shard_map/while/body/eval_jaxpr/ppermute | solution.py:12
  (16 other events, 4860.8 us)
Sparse Core Ops, SparseCore 0:
  10.2 824.3 all-gather.2
where the time goes:
time: 1660 us; the launch traced here: 1640 us
  waiting for transfers between devices  1080 us (65%)
  starting transfers between devices  334 us (20%)
  blocking collectives  114 us (7%)
  local copies, waits for them, and re-layouts  44.4 us (3%)
  matrix products  27.7 us (2%)
  other arithmetic  21.7 us (1%)
    all_gather x1, waiting for transfers between devices, shards(): drift_full = lax.all_gather(drift, ('slot', 'row'), axis=0, tiled=True)  823 us
    ppermute x32, starting transfers between devices, passed_along(): lax.ppermute(value, axis, [(source, source + steps) for source in range(i...  334 us
    ppermute x32, waiting for transfers between devices, passed_along(): lax.ppermute(value, axis, [(source, source + steps) for source in range(i...  259 us
    psum x1, blocking collectives, shards(): grads = lax.psum(partial_grads[None, :], 'row')  114 us
  transfers between devices with their start and end apart: 33, of which 17 were waited for; matrix products, arithmetic and copies ran while one was open for 0% of the time, Pallas kernels for 0%

commit v1 on v0

v1 whole, which is shorter than its diff:
```python
import jax
import jax.numpy as jnp
from jax import lax
from jax.experimental import pallas as pl
from jax.experimental.pallas import tpu as pltpu
from jax.sharding import PartitionSpec as P

ZL, X, Y, ZH, CORES = 4, 4, 4, 4, 2
BLOCK = 128
NB = 16
KEPT = NB // 2 + 1
PIECES = KEPT + 1
SLOTS = 16
CONTROLS = 16
BF = jnp.bfloat16


def source_of(index):
    r = index & 3
    zh = (index >> 2) & 3
    y = (index >> 4) & 3
    c = index >> 6
    return y * 32 + zh * 8 + c * 4 + r


def pick_matrix(dtype):
    rows = lax.broadcasted_iota(jnp.int32, (BLOCK, BLOCK), 0)
    cols = lax.broadcasted_iota(jnp.int32, (BLOCK, BLOCK), 1)
    return jnp.where(source_of(rows) == cols, 1.0, 0.0).astype(dtype)


def mm(a, b):
    return jnp.dot(a, b, preferred_element_type=jnp.float32)


def mm_t(a, b):
    return lax.dot_general(a, b, (((1,), (1,)), ((), ())), preferred_element_type=jnp.float32)


def at(start, size=BLOCK):
    return pl.ds(pl.multiple_of(start, size), size)


def chain_kernel(
    amps_ref, meta_ref, own_ref, other_ref, ctrl_ref, init_ref, target_ref, out_ref,
    even_h, odd_h, x_ref, pieces_ref, base_ref, work_ref,
):
    zl, xx = lax.axis_index("zl"), lax.axis_index("x")
    core = lax.axis_index("c")
    member = zl * X + xx
    backward = member >= SLOTS // 2
    lane = lax.rem(member, SLOTS // 2)
    pick = pick_matrix(BF)

    def lay(block_row, _):
        base = block_row * BLOCK
        zl_of = lax.div(block_row, X)
        x_of = lax.rem(block_row, X)
        for step in range(KEPT):
            col = lax.rem(block_row + step, NB) * BLOCK
            for ref, half in ((own_ref, core), (other_ref, 1 - core)):
                tiles = [ref[x_of * Y + y, zl_of * PIECES + step] for y in range(Y)]
                rows = pl.ds(pl.multiple_of(base + half * 64, 64), 64)
                even_h[rows, at(col)] = jnp.concatenate(tiles, axis=0)
        return 0

    lax.fori_loop(0, NB, lay, 0)
    eye = jnp.where(
        lax.broadcasted_iota(jnp.int32, (BLOCK, BLOCK), 0)
        == lax.broadcasted_iota(jnp.int32, (BLOCK, BLOCK), 1),
        1.0,
        0.0,
    ).astype(BF)

    def mirror(block_row, _):
        for step in range(1, NB // 2):
            other_row = lax.rem(block_row + step, NB) * BLOCK
            turned = mm_t(eye, even_h[at(block_row * BLOCK), at(other_row)])
            even_h[at(other_row), at(block_row * BLOCK)] = turned.astype(BF)
        return 0

    lax.fori_loop(0, NB, mirror, 0)

    def copy(block_row, _):
        odd_h[at(block_row * BLOCK), :] = even_h[at(block_row * BLOCK), :]
        return 0

    lax.fori_loop(0, NB, copy, 0)

    for k in range(CONTROLS):
        turned = mm(pick, ctrl_ref[k]).astype(BF)
        pieces_ref[k] = mm_t(turned, pick).astype(BF)
        pieces_ref[CONTROLS + k] = mm_t(pick, turned).astype(BF)

    def gather_base(p, _):
        base_ref[p] = even_h[at(meta_ref[0, p]), at(meta_ref[1, p])].astype(jnp.float32)
        return 0

    lax.fori_loop(0, 2 * CONTROLS, gather_base, 0)

    def scaled(p, slot):
        lead = meta_ref[2, p]
        start = jnp.where(lead == p, base_ref[p], work_ref[lead])
        amp = amps_ref[slot, p % CONTROLS]
        work_ref[lead] = start + amp * pieces_ref[p].astype(jnp.float32)

    def placed(p, target):
        value = work_ref[meta_ref[2, p]].astype(BF)
        target[at(meta_ref[0, p]), at(meta_ref[1, p])] = value

    def slot_of(step):
        return jnp.where(backward, SLOTS - 1 - step, step)

    def build(step, target):
        slot = slot_of(jnp.minimum(step, SLOTS - 1))
        for p in range(2 * CONTROLS):
            scaled(p, slot)
        for p in range(2 * CONTROLS):
            placed(p, target)

    x_ref[...] = jnp.zeros_like(x_ref)

    def load_from(ref):
        for part in range(2):
            for half in range(2):
                row = part * 4 + half
                x_ref[row : row + 1, :] = ref[part, pl.ds(lane + half * 8, 1), :]

    @pl.when(backward)
    def _():
        load_from(target_ref)

    @pl.when(jnp.logical_not(backward))
    def _():
        load_from(init_ref)

    for block in range(NB):
        cols = slice(block * BLOCK, (block + 1) * BLOCK)
        value = x_ref[:, cols]
        high = value.astype(BF)
        rest = value - high.astype(jnp.float32)
        middle = rest.astype(BF)
        low = (rest - middle.astype(jnp.float32)).astype(BF)
        x_ref[:, cols] = mm_t(high, pick) + mm_t(middle, pick) + mm_t(low, pick)

    def write(place):
        for quad in range(NB // 4):
            halves = []
            for pair in (2 * quad, 2 * quad + 1):
                first = x_ref[:, 2 * pair * BLOCK : (2 * pair + 1) * BLOCK]
                second = x_ref[:, (2 * pair + 1) * BLOCK : (2 * pair + 2) * BLOCK]
                halves.append(first + pltpu.roll(second, 2, axis=0))
            out_ref[place, quad * 16 : (quad + 1) * 16, :] = jnp.concatenate(halves, axis=0).astype(BF)

    @pl.when(backward)
    def _():
        write(SLOTS - 1)

    row_of = lax.broadcasted_iota(jnp.int32, (8, NB * BLOCK), 0)
    sign = jnp.where((row_of < 4) == jnp.logical_not(backward), 1.0, -1.0)

    def applied(values, ham):
        rounded = values.astype(BF)
        return jnp.concatenate(
            [mm(rounded, ham[:, n * 256 : (n + 1) * 256]) for n in range(NB // 2)], axis=1
        )

    def advance(step, ham):
        start = x_ref[...]
        u1 = applied(start, ham)
        u2 = applied(u1, ham) * (1.0 / 2)
        u3 = applied(u2, ham) * (1.0 / 3)
        u4 = applied(u3, ham) * (1.0 / 4)
        x_ref[...] = (start - u2 + u4) + sign * pltpu.roll(u1 - u3, 4, axis=0)
        place = jnp.where(backward, SLOTS - 2 - step, step)

        @pl.when(place >= 0)
        def _():
            write(place)

    build(0, even_h)

    def two_slots(pair, _):
        build(2 * pair + 1, odd_h)
        advance(2 * pair, even_h)
        build(2 * pair + 2, even_h)
        advance(2 * pair + 1, odd_h)
        return 0

    lax.fori_loop(0, SLOTS // 2, two_slots, 0)


def vmem():
    return pl.BlockSpec(memory_space=pltpu.VMEM)


def smem():
    return pl.BlockSpec(memory_space=pltpu.SMEM)


def chain(amps, meta, own, other, ctrl_blocks, init_states, targets):
    extent = NB * BLOCK
    return pl.pallas_call(
        chain_kernel,
        out_shape=jax.ShapeDtypeStruct((SLOTS, 64, BLOCK), BF),
        in_specs=[smem(), smem()] + [vmem()] * 5,
        out_specs=vmem(),
        scratch_shapes=[
            pltpu.VMEM((extent, extent), BF),
            pltpu.VMEM((extent, extent), BF),
            pltpu.VMEM((8, extent), jnp.float32),
            pltpu.VMEM((2 * CONTROLS, BLOCK, BLOCK), BF),
            pltpu.VMEM((2 * CONTROLS, BLOCK, BLOCK), jnp.float32),
            pltpu.VMEM((2 * CONTROLS, BLOCK, BLOCK), jnp.float32),
        ],
        compiler_params=pltpu.CompilerParams(vmem_limit_bytes=56 << 20),
        name="chain",
    )(amps, meta, own, other, ctrl_blocks, init_states, targets)


def finish_kernel(pos_ref, got_ref, ctrl_ref, states_ref, grads_ref, flat, left, right, sums):
    pick = pick_matrix(BF)
    for member in range(SLOTS):
        flat[member * 64 : (member + 1) * 64, :] = mm(got_ref[member], pick)
    for block in range(NB):
        pair, side = block // 2, block % 2
        cols = slice(block * BLOCK, (block + 1) * BLOCK)
        found = {}
        for which in range(2):
            for part in range(2):
                halves = []
                for half in range(2):
                    start = which * 512 + pair * 8 + part * 4 + side * 2 + half
                    value = flat[pl.ds(start, 8, stride=64), :]
                    if which == 0:
                        states_ref[part, half * 8 : (half + 1) * 8, cols] = value
                    halves.append(value)
                found[which, part] = jnp.concatenate(halves, axis=0)
        weights = [found[1, 0], found[1, 1]]
        source = [found[0, 1], -found[0, 0]]
        left[block] = jnp.concatenate(weights + source, axis=0).astype(BF)
        right[block] = jnp.concatenate(source + weights, axis=0)
    for k in range(CONTROLS):
        product = mm(left[pos_ref[k, 0]], ctrl_ref[k]) * right[pos_ref[k, 1]]
        sums[k : k + 1, :] = jnp.sum(product, axis=0, keepdims=True)
    ones = jnp.ones((8, BLOCK), jnp.float32)
    total = lax.dot_general(
        ones, sums[...], (((1,), (1,)), ((), ())),
        precision=lax.Precision.HIGHEST, preferred_element_type=jnp.float32,
    )
    grads_ref[...] = total[0:1, :] * (1.0 / 512)


def finish(pos, got, ctrl_blocks):
    return pl.pallas_call(
        finish_kernel,
        out_shape=(
            jax.ShapeDtypeStruct((2, 16, NB * BLOCK), jnp.float32),
            jax.ShapeDtypeStruct((1, CONTROLS), jnp.float32),
        ),
        in_specs=[smem(), vmem(), vmem()],
        out_specs=(vmem(), vmem()),
        scratch_shapes=[
            pltpu.VMEM((SLOTS * 64, BLOCK), jnp.float32),
            pltpu.VMEM((NB, 64, BLOCK), BF),
            pltpu.VMEM((NB, 64, BLOCK), jnp.float32),
            pltpu.VMEM((CONTROLS, BLOCK), jnp.float32),
        ],
        compiler_params=pltpu.CompilerParams(vmem_limit_bytes=32 << 20),
        name="finish",
    )(pos, got, ctrl_blocks)


def three_parts(values):
    high = lax.reduce_precision(values, 8, 7)
    middle = lax.reduce_precision(values - high, 8, 7)
    low = lax.reduce_precision(values - high - middle, 8, 7)
    return jnp.concatenate([high, middle, low, jnp.zeros_like(low)], axis=0).astype(BF)


def shared(values, axes, count):
    spread = jnp.broadcast_to(values[None], (count,) + values.shape)
    return lax.all_to_all(spread, axes, 0, 0)


def shards(drift, ctrl_blocks, blk_pos, amps, init_states, targets):
    member = lax.axis_index("zl") * X + lax.axis_index("x")
    twice = jnp.concatenate([drift, drift], axis=1)
    kept = lax.dynamic_slice(twice, (0, member * BLOCK), (4, KEPT * BLOCK))
    kept = jnp.einsum(
        "rjl,ml->jrm", kept.reshape(4, KEPT, BLOCK), pick_matrix(BF), preferred_element_type=BF
    )
    amps_rows = jnp.pad(three_parts(amps), ((0, 0), (0, BLOCK - CONTROLS)))
    packet = jnp.concatenate([kept, amps_rows[None]], axis=0)
    over_z = shared(packet, ("zl", "zh"), ZL * ZH)
    over_z = over_z.reshape(ZL, ZH, PIECES, 4, BLOCK).transpose(0, 2, 1, 3, 4)
    own = shared(over_z.reshape(ZL * PIECES, ZH * 4, BLOCK), ("x", "y"), X * Y)
    other = lax.ppermute(own, "c", [(0, 1), (1, 0)])
    sent = own.reshape(X, Y, ZL, PIECES, 16, BLOCK)[:, 0, :, KEPT, 0:3, 0:CONTROLS]
    amps_all = jnp.sum(sent.astype(jnp.float32), axis=2).transpose(1, 0, 2).reshape(SLOTS, CONTROLS)

    first, second = blk_pos[:, 0], blk_pos[:, 1]
    rows = jnp.concatenate([first, second])
    cols = jnp.concatenate([second, first])
    code = rows * NB + cols
    same = code[:, None] == code[None, :]
    lead = jnp.min(jnp.where(same, jnp.arange(2 * CONTROLS)[None, :], 2 * CONTROLS), axis=1)
    meta = jnp.stack([rows * BLOCK, cols * BLOCK, lead]).astype(jnp.int32)

    out = chain(amps_all, meta, own, other, ctrl_blocks, init_states, targets)
    got = lax.all_to_all(out, ("zl", "x"), 0, 0)
    states, partial_grads = finish(blk_pos, got, ctrl_blocks)
    grads = lax.psum(lax.psum(partial_grads, ("y", "c")), "zh")
    return states[None], grads


def solution(mesh):
    split = jax.sharding.Mesh(
        mesh.devices.reshape(ZL, X, Y, ZH, CORES), ("zl", "x", "y", "zh", "c")
    )
    slot, row = ("zl", "x"), ("y", "zh", "c")
    in_specs = (
        P(slot + row, None),
        P(),
        P(),
        P(slot, None),
        P(None, row, None),
        P(None, row, None),
    )
    out_specs = (P(slot, None, row, None), P(slot, None))
    return jax.shard_map(shards, mesh=split, in_specs=in_specs, out_specs=out_specs, check_vma=False)
```

time: 1660 us -> 233 us (0.14); the launches traced: 1640 us -> 233 us
  waiting for transfers between devices: 1080 us -> 12.8 us
  starting transfers between devices: 334 us -> 14.8 us
  Pallas kernels: 0 us -> 110 us
  local copies, waits for them, and re-layouts: 44.4 us -> 2.98 us
  matrix products: 27.7 us -> 0.2 us
  blocking collectives: 114 us -> 88.3 us
  other arithmetic: 21.7 us -> 2.47 us
    all_gather x1 -> x0, waiting for transfers between devices: 823 us -> none  [shards(): drift_full = lax.all_gather(drift, ('slot', 'row'), axis=0, tiled=True)]
    ppermute x32 -> x1, starting transfers between devices: 334 us -> 8.22 us  [shards(): other = lax.ppermute(own, 'c', [(0, 1), (1, 0)])]
    ppermute x32 -> x1, waiting for transfers between devices: 259 us -> 2.93 us  [shards(): other = lax.ppermute(own, 'c', [(0, 1), (1, 0)])]
    pallas_call x0 -> x2, Pallas kernels: none -> 110 us  [the longest x1 108 us: chain(): pl.pallas_call(chain_kernel, out_shape=jax.ShapeDtypeStruct((SLOTS, 64, B...]
    psum x1 -> x2, blocking collectives: 114 us -> 25.3 us  [shards(): grads = lax.psum(lax.psum(partial_grads, ('y', 'c')), 'zh')]
    all_to_all x0 -> x2, blocking collectives: none -> 63 us  [shared(): return lax.all_to_all(spread, axes, 0, 0)]
    dot_general x22 -> x1, matrix products: 27.7 us -> 0.2 us  [shards(): jnp.einsum('rjl,ml->jrm', kept.reshape(4, KEPT, BLOCK), pick_matrix(BF),...]
    another operation x32 -> x0, local copies, waits for them, and re-layouts: 22.1 us -> none
  transfers between devices with their start and end apart: 33 -> 2, of which waited for: 17 -> 2; matrix products, arithmetic and copies ran while one was open for 0% -> 1% of each run, Pallas kernels for 0% -> 0%
where the time goes in v1:
time: 233 us
  Pallas kernels  110 us (47%)
  blocking collectives  88.3 us (38%)
  starting transfers between devices  14.8 us (6%)
  waiting for transfers between devices  12.8 us (5%)
  local copies, waits for them, and re-layouts  2.98 us (1%)
  other arithmetic  2.47 us (1%)
    pallas_call x1, Pallas kernels, chain(): pl.pallas_call(chain_kernel, out_shape=jax.ShapeDtypeStruct((SLOTS, 64, B...  108 us
    all_to_all x2, blocking collectives, shared(): return lax.all_to_all(spread, axes, 0, 0)  63 us
    psum x2, blocking collectives, shards(): grads = lax.psum(lax.psum(partial_grads, ('y', 'c')), 'zh')  25.3 us
    all_to_all x1, waiting for transfers between devices, shards(): got = lax.all_to_all(out, ('zl', 'x'), 0, 0)  9.83 us
    ppermute x1, starting transfers between devices, shards(): other = lax.ppermute(own, 'c', [(0, 1), (1, 0)])  8.22 us
    all_to_all x1, starting transfers between devices, shards(): got = lax.all_to_all(out, ('zl', 'x'), 0, 0)  6.63 us
  transfers between devices with their start and end apart: 2, of which 2 were waited for; matrix products, arithmetic and copies ran while one was open for 1% of the time, Pallas kernels for 0%

profile of v1, /device:TPU:1, one launch (start us, length us, event | category | flops | bytes accessed | tf_op | source)
XLA Modules:
  0.0 232.8 jit_solution(4922093692858811708)
XLA Ops:
  0.7 0.7 fusion.5
  1.4 0.7 reduce-precision_convert_fusion.1
  2.1 0.1 pad.21.clone
  2.1 0.1 maximum_maximum_fusion
  2.2 0.2 convolution_bitcast_fusion
  2.5 27.9 %all_to_all.15 = bf16[16,10,4,128]{3,2,1,0:T(4,128)(2,1)S(1)} all-to-all(bf16[16,10,4,128]{3,2,1,0:T(4,128)(2,1)S(1)} %broadcast_in_dim.45), channel_id=1, replica_groups=mesh['zl'=4,'x'=4,'y'=4,'zh'=4,'c'=2] {'zl','zh'}, dimensions={0} | all-to-all | bytes 327680 | tf_op jit(solution)/shard_map/all_to_all | solution.py:283
  30.5 0.1 copy.26
  30.6 0.5 broadcast_in_dim.47
  31.1 35.2 %all_to_all.16.own_ref = bf16[16,40,16,128]{3,2,1,0:T(8,128)(2,1)S(1)} all-to-all(bf16[16,40,16,128]{3,2,1,0:T(8,128)(2,1)S(1)} %broadcast_in_dim.47), channel_id=1, replica_groups=mesh['zl'=4,'x'=4,'y'=4,'zh'=4,'c'=2] {'x','y'}, dimensions={0} | all-to-all | bytes 5242880 | tf_op jit(solution)/shard_map/all_to_all | solution.py:283
  66.2 8.2 %collective-permute-start = (bf16[16,40,16,128]{3,2,1,0:T(8,128)(2,1)S(1)}, bf16[16,40,16,128]{3,2,1,0:T(8,128)(2,1)S(1)}, u32[]{:S(2)}, u32[]{:S(2)}) collective-permute-start(bf16[16,40,16,128]{3,2,1,0:T(8,128)(2,1)S(1)} %all_to_all.16.own_ref), channel_id=1, source_target_pairs={{0,1},{1,0},{2,3},{3,2},{4,5},{5,4},{6,7},{7,6},{8,9},{9,8},{10,11... | collective-permute-start | bytes 7864328 | tf_op jit(solution)/shard_map/ppermute | solution.py:298
  74.5 0.1 fusion.16
  74.5 0.1 add_multiply_fusion
  74.6 0.2 select_reduce_fusion
  74.8 0.6 pad_add_fusion.meta_ref
  75.4 0.6 copy.27
  76.0 2.9 %collective-permute-done.other_ref = bf16[16,40,16,128]{3,2,1,0:T(8,128)(2,1)S(1)} collective-permute-done((bf16[16,40,16,128]{3,2,1,0:T(8,128)(2,1)S(1)}, bf16[16,40,16,128]{3,2,1,0:T(8,128)(2,1)S(1)}, u32[]{:S(2)}, u32[]{:S(2)}) %collective-permute-start) | collective-permute-done | bytes 2621472 | tf_op jit(solution)/shard_map/ppermute | solution.py:298
  79.0 1.5 copy-done.2
  80.5 108.3 %chain.1 = bf16[16,64,128]{2,1,0:T(8,128)(2,1)} custom-call(f32[16,16]{1,0:T(8,128)} %bitcast.29, s32[3,32]{1,0:T(4,128)} %pad_add_fusion.meta_ref, bf16[16,40,16,128]{3,2,1,0:T(8,128)(2,1)} %copy-done.1, bf16[16,40,16,128]{3,2,1,0:T(8,128)(2,1)} %copy-done.2, bf16[16,128,128]{2,1,0:T(8,128)(2,1)} %ctrl_ref.3, f32[2,16,2048]{2,1,0:T(8,128)} %init_ref.1, ...), custom_call_target="tpu_custom_call" | custom-call | tf_op jit(solution)/shard_map/chain/pallas_call | solution.py:203
  188.8 6.6 %all-to-all-start.2 = ((bf16[16,64,128]{2,1,0:T(8,128)(2,1)}), bf16[16,64,128]{2,1,0:T(8,128)(2,1)S(1)}, u32[]{:S(2)}, u32[]{:S(2)}) async-start(bf16[16,64,128]{2,1,0:T(8,128)(2,1)} %chain.1), calls=%async_computation.2 | async-start | bytes 524288 | tf_op jit(solution)/shard_map/all_to_all | solution.py:311
  195.5 0.1 copy.28.pos_ref
  195.5 9.8 %all-to-all-done.2.got_ref = bf16[16,64,128]{2,1,0:T(8,128)(2,1)S(1)} async-done(((bf16[16,64,128]{2,1,0:T(8,128)(2,1)}), bf16[16,64,128]{2,1,0:T(8,128)(2,1)S(1)}, u32[]{:S(2)}, u32[]{:S(2)}) %all-to-all-start.2) | async-done | bytes 262176 | tf_op jit(solution)/shard_map/all_to_all | solution.py:311
  205.4 2.1 finish.1
  207.5 13.5 %psum.14 = f32[1,16]{1,0:T(1,128)S(1)} all-reduce(f32[1,16]{1,0:T(1,128)S(1)} %get-tuple-element.5), channel_id=1, replica_groups=mesh['zl'=4,'x'=4,'y'=4,'zh'=4,'c'=2] {'y','c'}, use_global_device_ids=true, to_apply=%region_2.3 | all-reduce | flops 16 | bytes 128 | tf_op jit(solution)/shard_map/psum | solution.py:313
  221.0 11.8 %psum.15 = f32[1,16]{1,0:T(1,128)} all-reduce(f32[1,16]{1,0:T(1,128)S(1)} %psum.14), channel_id=1, replica_groups=mesh['zl'=4,'x'=4,'y'=4,'zh'=4,'c'=2] {'zh'}, use_global_device_ids=true, to_apply=%region_3.4 | all-reduce | flops 16 | bytes 128 | tf_op jit(solution)/shard_map/psum | solution.py:313
  (17 shorter events, 0.2 us)
Async XLA Ops:
  31.1 43.4 %copy-start.3 = (s32[16,2]{0,1:T(2,128)S(1)}, s32[16,2]{0,1:T(2,128)}, u32[]{:S(2)}) copy-start(s32[16,2]{0,1:T(2,128)} %param.8) | copy-start | bytes 388
  66.2 12.7 %copy-start.1 = (bf16[16,40,16,128]{3,2,1,0:T(8,128)(2,1)}, bf16[16,40,16,128]{3,2,1,0:T(8,128)(2,1)S(1)}, u32[]{:S(2)}) copy-start(bf16[16,40,16,128]{3,2,1,0:T(8,128)(2,1)S(1)} %all_to_all.16.own_ref) | copy-start | bytes 7864324
  66.2 12.7 %collective-permute-start = (bf16[16,40,16,128]{3,2,1,0:T(8,128)(2,1)S(1)}, bf16[16,40,16,128]{3,2,1,0:T(8,128)(2,1)S(1)}, u32[]{:S(2)}, u32[]{:S(2)}) collective-permute-start(bf16[16,40,16,128]{3,2,1,0:T(8,128)(2,1)S(1)} %all_to_all.16.own_ref), channel_id=1, source_target_pairs={{0,1},{1,0},{2,3},{3,2},{4,5},{5,4},{6,7},{7,6},{8,9},{9,8},{10,11... | collective-permute-start | bytes 7864328 | tf_op jit(solution)/shard_map/ppermute | solution.py:298
  79.0 1.5 copy-start.2
  80.5 124.9 %copy-start = (bf16[16,128,128]{2,1,0:T(8,128)(2,1)S(1)}, bf16[16,128,128]{2,1,0:T(8,128)(2,1)}, u32[]{:S(2)}) copy-start(bf16[16,128,128]{2,1,0:T(8,128)(2,1)} %ctrl_ref.3) | copy-start | bytes 1572868
  188.8 16.6 %all-to-all-start.2 = ((bf16[16,64,128]{2,1,0:T(8,128)(2,1)}), bf16[16,64,128]{2,1,0:T(8,128)(2,1)S(1)}, u32[]{:S(2)}, u32[]{:S(2)}) async-start(bf16[16,64,128]{2,1,0:T(8,128)(2,1)} %chain.1), calls=%async_computation.2 | async-start | bytes 524288 | tf_op jit(solution)/shard_map/all_to_all | solution.py:311

commit v2 on v1

--- a/solution.py
+++ b/solution.py
@@ -1,3 +1,5 @@
+import functools
+
 import jax
 import jax.numpy as jnp
 from jax import lax
@@ -41,16 +43,52 @@
     return pl.ds(pl.multiple_of(start, size), size)
 
 
-def chain_kernel(
-    amps_ref, meta_ref, own_ref, other_ref, ctrl_ref, init_ref, target_ref, out_ref,
-    even_h, odd_h, x_ref, pieces_ref, base_ref, work_ref,
-):
-    zl, xx = lax.axis_index("zl"), lax.axis_index("x")
-    core = lax.axis_index("c")
-    member = zl * X + xx
+def this_member():
+    return lax.axis_index("zl") * X + lax.axis_index("x")
+
+
+def prepare_kernel(ctrl_ref, init_ref, target_ref, pieces_ref, begin_ref):
+    member = this_member()
     backward = member >= SLOTS // 2
     lane = lax.rem(member, SLOTS // 2)
     pick = pick_matrix(BF)
+    for k in range(CONTROLS):
+        turned = mm(pick, ctrl_ref[k]).astype(BF)
+        pieces_ref[k] = mm_t(turned, pick).astype(BF)
+        pieces_ref[CONTROLS + k] = mm_t(pick, turned).astype(BF)
+
+    begin_ref[...] = jnp.zeros_like(begin_ref)
+
+    def load_from(ref):
+        for part in range(2):
+            for half in range(2):
+                row = part * 4 + half
+                begin_ref[row : row + 1, :] = ref[part, pl.ds(lane + half * 8, 1), :]
+
+    @pl.when(backward)
+    def _():
+        load_from(target_ref)
+
+    @pl.when(jnp.logical_not(backward))
+    def _():
+        load_from(init_ref)
+
+    for block in range(NB):
+        cols = slice(block * BLOCK, (block + 1) * BLOCK)
+        value = begin_ref[:, cols]
+        high = value.astype(BF)
+        rest = value - high.astype(jnp.float32)
+        middle = rest.astype(BF)
+        low = (rest - middle.astype(jnp.float32)).astype(BF)
+        begin_ref[:, cols] = mm_t(high, pick) + mm_t(middle, pick) + mm_t(low, pick)
+
+
+def chain_kernel(
+    amps_ref, meta_ref, own_ref, other_ref, pieces_ref, begin_ref, out_ref,
+    even_h, odd_h, x_ref, base_ref, work_ref,
+):
+    core = lax.axis_index("c")
+    backward = this_member() >= SLOTS // 2
 
     def lay(block_row, _):
         base = block_row * BLOCK
@@ -58,49 +96,31 @@
         x_of = lax.rem(block_row, X)
         for step in range(KEPT):
             col = lax.rem(block_row + step, NB) * BLOCK
-            for ref, half in ((own_ref, core), (other_ref, 1 - core)):
-                tiles = [ref[x_of * Y + y, zl_of * PIECES + step] for y in range(Y)]
-                rows = pl.ds(pl.multiple_of(base + half * 64, 64), 64)
-                even_h[rows, at(col)] = jnp.concatenate(tiles, axis=0)
+            mine, theirs = (
+                jnp.concatenate([ref[x_of * Y + y, zl_of * PIECES + step] for y in range(Y)], axis=0)
+                for ref in (own_ref, other_ref)
+            )
+            first = jnp.where(core == 0, mine, theirs)
+            second = jnp.where(core == 0, theirs, mine)
+            block = jnp.concatenate([first, second], axis=0)
+            turned = block.T if 0 < step < NB // 2 else None
+            for ham in (even_h, odd_h):
+                ham[at(base), at(col)] = block
+                if turned is not None:
+                    ham[at(col), at(base)] = turned
         return 0
 
     lax.fori_loop(0, NB, lay, 0)
-    eye = jnp.where(
-        lax.broadcasted_iota(jnp.int32, (BLOCK, BLOCK), 0)
-        == lax.broadcasted_iota(jnp.int32, (BLOCK, BLOCK), 1),
-        1.0,
-        0.0,
-    ).astype(BF)
-
-    def mirror(block_row, _):
-        for step in range(1, NB // 2):
-            other_row = lax.rem(block_row + step, NB) * BLOCK
-            turned = mm_t(eye, even_h[at(block_row * BLOCK), at(other_row)])
-            even_h[at(other_row), at(block_row * BLOCK)] = turned.astype(BF)
-        return 0
-
-    lax.fori_loop(0, NB, mirror, 0)
-
-    def copy(block_row, _):
-        odd_h[at(block_row * BLOCK), :] = even_h[at(block_row * BLOCK), :]
-        return 0
-
-    lax.fori_loop(0, NB, copy, 0)
-
-    for k in range(CONTROLS):
-        turned = mm(pick, ctrl_ref[k]).astype(BF)
-        pieces_ref[k] = mm_t(turned, pick).astype(BF)
-        pieces_ref[CONTROLS + k] = mm_t(pick, turned).astype(BF)
 
     def gather_base(p, _):
-        base_ref[p] = even_h[at(meta_ref[0, p]), at(meta_ref[1, p])].astype(jnp.float32)
+        base_ref[p] = even_h[at(meta_ref[0, p]), at(meta_ref[1, p])]
         return 0
 
     lax.fori_loop(0, 2 * CONTROLS, gather_base, 0)
 
     def scaled(p, slot):
         lead = meta_ref[2, p]
-        start = jnp.where(lead == p, base_ref[p], work_ref[lead])
+        start = jnp.where(lead == p, base_ref[p].astype(jnp.float32), work_ref[lead])
         amp = amps_ref[slot, p % CONTROLS]
         work_ref[lead] = start + amp * pieces_ref[p].astype(jnp.float32)
 
@@ -111,37 +131,13 @@
     def slot_of(step):
         return jnp.where(backward, SLOTS - 1 - step, step)
 
-    def build(step, target):
+    def tasks(step, target):
         slot = slot_of(jnp.minimum(step, SLOTS - 1))
-        for p in range(2 * CONTROLS):
-            scaled(p, slot)
-        for p in range(2 * CONTROLS):
-            placed(p, target)
-
-    x_ref[...] = jnp.zeros_like(x_ref)
-
-    def load_from(ref):
-        for part in range(2):
-            for half in range(2):
-                row = part * 4 + half
-                x_ref[row : row + 1, :] = ref[part, pl.ds(lane + half * 8, 1), :]
-
-    @pl.when(backward)
-    def _():
-        load_from(target_ref)
-
-    @pl.when(jnp.logical_not(backward))
-    def _():
-        load_from(init_ref)
-
-    for block in range(NB):
-        cols = slice(block * BLOCK, (block + 1) * BLOCK)
-        value = x_ref[:, cols]
-        high = value.astype(BF)
-        rest = value - high.astype(jnp.float32)
-        middle = rest.astype(BF)
-        low = (rest - middle.astype(jnp.float32)).astype(BF)
-        x_ref[:, cols] = mm_t(high, pick) + mm_t(middle, pick) + mm_t(low, pick)
+        adds = [functools.partial(scaled, p, slot) for p in range(2 * CONTROLS)]
+        puts = [functools.partial(placed, p, target) for p in range(2 * CONTROLS)]
+        return adds + puts
+
+    x_ref[...] = begin_ref[...]
 
     def write(place):
         for quad in range(NB // 4):
@@ -159,18 +155,22 @@
     row_of = lax.broadcasted_iota(jnp.int32, (8, NB * BLOCK), 0)
     sign = jnp.where((row_of < 4) == jnp.logical_not(backward), 1.0, -1.0)
 
-    def applied(values, ham):
+    def applied(values, ham, todo):
         rounded = values.astype(BF)
-        return jnp.concatenate(
-            [mm(rounded, ham[:, n * 256 : (n + 1) * 256]) for n in range(NB // 2)], axis=1
-        )
-
-    def advance(step, ham):
+        found = []
+        for n in range(NB // 2):
+            found.append(mm(rounded, ham[:, n * 256 : (n + 1) * 256]))
+            for task in todo[2 * n : 2 * n + 2]:
+                task()
+        return jnp.concatenate(found, axis=1)
+
+    def advance(step, ham, following):
+        todo = tasks(step + 1, following)
         start = x_ref[...]
-        u1 = applied(start, ham)
-        u2 = applied(u1, ham) * (1.0 / 2)
-        u3 = applied(u2, ham) * (1.0 / 3)
-        u4 = applied(u3, ham) * (1.0 / 4)
+        u1 = applied(start, ham, todo[0:16])
+        u2 = applied(u1, ham, todo[16:32]) * (1.0 / 2)
+        u3 = applied(u2, ham, todo[32:48]) * (1.0 / 3)
+        u4 = applied(u3, ham, todo[48:64]) * (1.0 / 4)
         x_ref[...] = (start - u2 + u4) + sign * pltpu.roll(u1 - u3, 4, axis=0)
         place = jnp.where(backward, SLOTS - 2 - step, step)
 
@@ -178,13 +178,12 @@
         def _():
             write(place)
 
-    build(0, even_h)
+    for task in tasks(0, even_h):
+        task()
 
     def two_slots(pair, _):
-        build(2 * pair + 1, odd_h)
-        advance(2 * pair, even_h)
-        build(2 * pair + 2, even_h)
-        advance(2 * pair + 1, odd_h)
+        advance(2 * pair, even_h, odd_h)
+        advance(2 * pair + 1, odd_h, even_h)
         return 0
 
     lax.fori_loop(0, SLOTS // 2, two_slots, 0)
@@ -198,12 +197,29 @@
     return pl.BlockSpec(memory_space=pltpu.SMEM)
 
 
-def chain(amps, meta, own, other, ctrl_blocks, init_states, targets):
+def prepare(ctrl_blocks, init_states, targets):
+    return pl.pallas_call(
+        prepare_kernel,
+        out_shape=(
+            jax.ShapeDtypeStruct((2 * CONTROLS, BLOCK, BLOCK), BF),
+            jax.ShapeDtypeStruct((8, NB * BLOCK), jnp.float32),
+        ),
+        in_specs=[vmem()] * 3,
+        out_specs=(vmem(), vmem()),
+        compiler_params=pltpu.CompilerParams(vmem_limit_bytes=16 << 20),
+        cost_estimate=pl.CostEstimate(
+            flops=2 * 3 * CONTROLS * BLOCK**3, bytes_accessed=8 << 20, transcendentals=0
+        ),
+        name="prepare",
+    )(ctrl_blocks, init_states, targets)
+
+
+def chain(amps, meta, own, other, pieces, begin):
     extent = NB * BLOCK
     return pl.pallas_call(
         chain_kernel,
         out_shape=jax.ShapeDtypeStruct((SLOTS, 64, BLOCK), BF),
-        in_specs=[smem(), smem()] + [vmem()] * 5,
+        in_specs=[smem(), smem()] + [vmem()] * 4,
         out_specs=vmem(),
         scratch_shapes=[
             pltpu.VMEM((extent, extent), BF),
@@ -211,11 +227,13 @@
             pltpu.VMEM((8, extent), jnp.float32),
             pltpu.VMEM((2 * CONTROLS, BLOCK, BLOCK), BF),
             pltpu.VMEM((2 * CONTROLS, BLOCK, BLOCK), jnp.float32),
-            pltpu.VMEM((2 * CONTROLS, BLOCK, BLOCK), jnp.float32),
         ],
-        compiler_params=pltpu.CompilerParams(vmem_limit_bytes=56 << 20),
+        compiler_params=pltpu.CompilerParams(vmem_limit_bytes=30 << 20),
+        cost_estimate=pl.CostEstimate(
+            flops=2 * 8 * 64 * extent**2, bytes_accessed=8 << 20, transcendentals=0
+        ),
         name="chain",
-    )(amps, meta, own, other, ctrl_blocks, init_states, targets)
+    )(amps, meta, own, other, pieces, begin)
 
 
 def finish_kernel(pos_ref, got_ref, ctrl_ref, states_ref, grads_ref, flat, left, right, sums):
@@ -284,7 +302,8 @@
 
 
 def shards(drift, ctrl_blocks, blk_pos, amps, init_states, targets):
-    member = lax.axis_index("zl") * X + lax.axis_index("x")
+    member = this_member()
+    pieces, begin = prepare(ctrl_blocks, init_states, targets)
     twice = jnp.concatenate([drift, drift], axis=1)
     kept = lax.dynamic_slice(twice, (0, member * BLOCK), (4, KEPT * BLOCK))
     kept = jnp.einsum(
@@ -307,7 +326,7 @@
     lead = jnp.min(jnp.where(same, jnp.arange(2 * CONTROLS)[None, :], 2 * CONTROLS), axis=1)
     meta = jnp.stack([rows * BLOCK, cols * BLOCK, lead]).astype(jnp.int32)
 
-    out = chain(amps_all, meta, own, other, ctrl_blocks, init_states, targets)
+    out = chain(amps_all, meta, own, other, pieces, begin)
     got = lax.all_to_all(out, ("zl", "x"), 0, 0)
     states, partial_grads = finish(blk_pos, got, ctrl_blocks)
     grads = lax.psum(lax.psum(partial_grads, ("y", "c")), "zh")

time: 233 us -> 205 us (0.88)
  Pallas kernels: 110 us -> 86.9 us
    pallas_call x1, Pallas kernels: 108 us -> 81.5 us  [chain(): pl.pallas_call(chain_kernel, out_shape=jax.ShapeDtypeStruct((SLOTS, 64, B...]
    pallas_call x0 -> x1, Pallas kernels: none -> 3.23 us  [prepare(): pl.pallas_call(prepare_kernel, out_shape=(jax.ShapeDtypeStruct((2 * CONTR...]
  transfers between devices with their start and end apart: 2 -> 2, of which waited for: 2 -> 2; matrix products, arithmetic and copies ran while one was open for 1% -> 0% of each run, Pallas kernels for 0% -> 2%
where the time goes in v2:
time: 205 us
  blocking collectives  88.5 us (43%)
  Pallas kernels  86.9 us (42%)
  starting transfers between devices  14.8 us (7%)
  waiting for transfers between devices  10.6 us (5%)
    pallas_call x1, Pallas kernels, chain(): pl.pallas_call(chain_kernel, out_shape=jax.ShapeDtypeStruct((SLOTS, 64, B...  81.5 us
    all_to_all x2, blocking collectives, shared(): return lax.all_to_all(spread, axes, 0, 0)  63.2 us
    psum x2, blocking collectives, shards(): grads = lax.psum(lax.psum(partial_grads, ('y', 'c')), 'zh')  25.3 us
    all_to_all x1, waiting for transfers between devices, shards(): got = lax.all_to_all(out, ('zl', 'x'), 0, 0)  9.83 us
    ppermute x1, starting transfers between devices, shards(): other = lax.ppermute(own, 'c', [(0, 1), (1, 0)])  8.22 us
    all_to_all x1, starting transfers between devices, shards(): got = lax.all_to_all(out, ('zl', 'x'), 0, 0)  6.62 us
  transfers between devices with their start and end apart: 2, of which 2 were waited for; matrix products, arithmetic and copies ran while one was open for 0% of the time, Pallas kernels for 2%

profile of v2, /device:TPU:1, one launch (start us, length us, event | category | flops | bytes accessed | tf_op | source)
XLA Modules:
  0.0 204.6 jit_solution(4395448840739522849)
XLA Ops:
  0.7 0.7 fusion.5
  1.4 0.7 reduce-precision_convert_fusion.1
  2.1 0.1 pad.21.clone
  2.1 0.1 maximum_maximum_fusion
  2.2 0.2 convolution_bitcast_fusion
  2.5 27.9 %all_to_all.15 = bf16[16,10,4,128]{3,2,1,0:T(4,128)(2,1)S(1)} all-to-all(bf16[16,10,4,128]{3,2,1,0:T(4,128)(2,1)S(1)} %broadcast_in_dim.45), channel_id=1, replica_groups=mesh['zl'=4,'x'=4,'y'=4,'zh'=4,'c'=2] {'zl','zh'}, dimensions={0} | all-to-all | bytes 327680 | tf_op jit(solution)/shard_map/all_to_all | solution.py:301
  30.5 0.1 copy.26
  30.6 0.5 broadcast_in_dim.47
  31.1 0.0 copy-start
  31.1 0.0 copy-start.1
  31.1 35.3 %all_to_all.16.own_ref = bf16[16,40,16,128]{3,2,1,0:T(8,128)(2,1)S(1)} all-to-all(bf16[16,40,16,128]{3,2,1,0:T(8,128)(2,1)S(1)} %broadcast_in_dim.47), channel_id=1, replica_groups=mesh['zl'=4,'x'=4,'y'=4,'zh'=4,'c'=2] {'x','y'}, dimensions={0} | all-to-all | bytes 5242880 | tf_op jit(solution)/shard_map/all_to_all | solution.py:301
  66.4 8.2 %collective-permute-start = (bf16[16,40,16,128]{3,2,1,0:T(8,128)(2,1)S(1)}, bf16[16,40,16,128]{3,2,1,0:T(8,128)(2,1)S(1)}, u32[]{:S(2)}, u32[]{:S(2)}) collective-permute-start(bf16[16,40,16,128]{3,2,1,0:T(8,128)(2,1)S(1)} %all_to_all.16.own_ref), channel_id=1, source_target_pairs={{0,1},{1,0},{2,3},{3,2},{4,5},{5,4},{6,7},{7,6},{8,9},{9,8},{10,11... | collective-permute-start | bytes 7864328 | tf_op jit(solution)/shard_map/ppermute | solution.py:317
  74.6 3.2 %prepare.1 = (bf16[32,128,128]{2,1,0:T(8,128)(2,1)S(1)}, f32[8,2048]{1,0:T(8,128)S(1)}) custom-call(bf16[16,128,128]{2,1,0:T(8,128)(2,1)S(1)} %copy-done, f32[2,16,2048]{2,1,0:T(8,128)S(1)} %copy-done.1, f32[2,16,2048]{2,1,0:T(8,128)S(1)} %copy-done.2), custom_call_target="tpu_custom_call" | custom-call | flops 201326592 | bytes 8388608 | tf_op jit(solution)/shard_map/prepare/pallas_call | solution.py:201
  77.9 0.1 fusion.16
  78.0 0.1 add_multiply_fusion
  78.1 0.2 select_reduce_fusion
  78.3 0.8 collective-permute-done.other_ref
  79.1 81.5 %chain.1 = bf16[16,64,128]{2,1,0:T(8,128)(2,1)} custom-call(f32[16,16]{1,0:T(8,128)S(1)} %bitcast.27, s32[3,32]{1,0:T(4,128)S(1)} %pad_add_fusion.meta_ref, bf16[16,40,16,128]{3,2,1,0:T(8,128)(2,1)S(1)} %all_to_all.16.own_ref, bf16[16,40,16,128]{3,2,1,0:T(8,128)(2,1)S(1)} %collective-permute-done.other_ref, ...), custom_call_target="tpu_custom_call" | custom-call | flops 4294967296 | bytes 8388608 | tf_op jit(solution)/shard_map/chain/pallas_call | solution.py:219
  160.6 6.6 %all-to-all-start.2 = ((bf16[16,64,128]{2,1,0:T(8,128)(2,1)}), bf16[16,64,128]{2,1,0:T(8,128)(2,1)S(1)}, u32[]{:S(2)}, u32[]{:S(2)}) async-start(bf16[16,64,128]{2,1,0:T(8,128)(2,1)} %chain.1), calls=%async_computation.2 | async-start | bytes 524288 | tf_op jit(solution)/shard_map/all_to_all | solution.py:330
  167.3 0.1 copy.28.pos_ref
  167.3 9.8 %all-to-all-done.2.got_ref = bf16[16,64,128]{2,1,0:T(8,128)(2,1)S(1)} async-done(((bf16[16,64,128]{2,1,0:T(8,128)(2,1)}), bf16[16,64,128]{2,1,0:T(8,128)(2,1)S(1)}, u32[]{:S(2)}, u32[]{:S(2)}) %all-to-all-start.2) | async-done | bytes 262176 | tf_op jit(solution)/shard_map/all_to_all | solution.py:330
  177.2 2.1 %finish.1 = (f32[2,16,2048]{2,1,0:T(8,128)}, f32[1,16]{1,0:T(1,128)S(1)}) custom-call(s32[16,2]{1,0:T(8,128)S(1)} %copy.28.pos_ref, bf16[16,64,128]{2,1,0:T(8,128)(2,1)S(1)} %all-to-all-done.2.got_ref, bf16[16,128,128]{2,1,0:T(8,128)(2,1)S(1)} %copy-done), custom_call_target="tpu_custom_call" | custom-call | tf_op jit(solution)/shard_map/finish/pallas_call | solution.py:273
  179.3 13.5 %psum.14 = f32[1,16]{1,0:T(1,128)S(1)} all-reduce(f32[1,16]{1,0:T(1,128)S(1)} %get-tuple-element.9), channel_id=1, replica_groups=mesh['zl'=4,'x'=4,'y'=4,'zh'=4,'c'=2] {'y','c'}, use_global_device_ids=true, to_apply=%region_2.3 | all-reduce | flops 16 | bytes 128 | tf_op jit(solution)/shard_map/psum | solution.py:332
  192.8 11.8 %psum.15 = f32[1,16]{1,0:T(1,128)} all-reduce(f32[1,16]{1,0:T(1,128)S(1)} %psum.14), channel_id=1, replica_groups=mesh['zl'=4,'x'=4,'y'=4,'zh'=4,'c'=2] {'zh'}, use_global_device_ids=true, to_apply=%region_3.4 | all-reduce | flops 16 | bytes 128 | tf_op jit(solution)/shard_map/psum | solution.py:332
  (18 shorter events, 0.2 us)
Async XLA Ops:
  31.1 43.6 %copy-start = (bf16[16,128,128]{2,1,0:T(8,128)(2,1)S(1)}, bf16[16,128,128]{2,1,0:T(8,128)(2,1)}, u32[]{:S(2)}) copy-start(bf16[16,128,128]{2,1,0:T(8,128)(2,1)} %ctrl_ref.3) | copy-start | bytes 1572868
  31.1 43.6 %copy-start.1 = (f32[2,16,2048]{2,1,0:T(8,128)S(1)}, f32[2,16,2048]{2,1,0:T(8,128)}, u32[]{:S(2)}) copy-start(f32[2,16,2048]{2,1,0:T(8,128)} %init_ref.1) | copy-start | bytes 786436
  31.1 43.6 %copy-start.2 = (f32[2,16,2048]{2,1,0:T(8,128)S(1)}, f32[2,16,2048]{2,1,0:T(8,128)}, u32[]{:S(2)}) copy-start(f32[2,16,2048]{2,1,0:T(8,128)} %target_ref.1) | copy-start | bytes 786436
  31.1 46.8 %copy-start.3 = (s32[16,2]{0,1:T(2,128)S(1)}, s32[16,2]{0,1:T(2,128)}, u32[]{:S(2)}) copy-start(s32[16,2]{0,1:T(2,128)} %param.8) | copy-start | bytes 388
  66.4 12.7 %collective-permute-start = (bf16[16,40,16,128]{3,2,1,0:T(8,128)(2,1)S(1)}, bf16[16,40,16,128]{3,2,1,0:T(8,128)(2,1)S(1)}, u32[]{:S(2)}, u32[]{:S(2)}) collective-permute-start(bf16[16,40,16,128]{3,2,1,0:T(8,128)(2,1)S(1)} %all_to_all.16.own_ref), channel_id=1, source_target_pairs={{0,1},{1,0},{2,3},{3,2},{4,5},{5,4},{6,7},{7,6},{8,9},{9,8},{10,11... | collective-permute-start | bytes 7864328 | tf_op jit(solution)/shard_map/ppermute | solution.py:317
  160.6 16.5 %all-to-all-start.2 = ((bf16[16,64,128]{2,1,0:T(8,128)(2,1)}), bf16[16,64,128]{2,1,0:T(8,128)(2,1)S(1)}, u32[]{:S(2)}, u32[]{:S(2)}) async-start(bf16[16,64,128]{2,1,0:T(8,128)(2,1)} %chain.1), calls=%async_computation.2 | async-start | bytes 524288 | tf_op jit(solution)/shard_map/all_to_all | solution.py:330

commit v3 on v2

--- a/solution.py
+++ b/solution.py
@@ -11,7 +11,7 @@
 BLOCK = 128
 NB = 16
 KEPT = NB // 2 + 1
-PIECES = KEPT + 1
+HALF = BLOCK // 2
 SLOTS = 16
 CONTROLS = 16
 BF = jnp.bfloat16
@@ -45,6 +45,29 @@
 
 def this_member():
     return lax.axis_index("zl") * X + lax.axis_index("x")
+
+
+def kept_half(member, core):
+    return jnp.where(member < SLOTS // 2, core, 1 - core)
+
+
+def source_kernel(drift_ref, amps_ref, packet_ref):
+    member = this_member()
+    pick = pick_matrix(BF)
+    for step in range(KEPT - 1):
+        block = lax.rem(member + step, NB)
+        packet_ref[step] = mm_t(drift_ref[:, at(block * BLOCK)], pick).astype(BF)
+    block = lax.rem(member + KEPT - 1, NB)
+    kept = mm_t(drift_ref[:, at(block * BLOCK)], pick)
+    row = lax.broadcasted_iota(jnp.int32, (4, BLOCK), 0)
+    lane = lax.broadcasted_iota(jnp.int32, (4, BLOCK), 1)
+    amps = amps_ref[...]
+    high = amps.astype(BF).astype(jnp.float32)
+    middle = (amps - high).astype(BF).astype(jnp.float32)
+    low = amps - high - middle
+    parts = jnp.where(row == 0, high, jnp.where(row == 1, middle, jnp.where(row == 2, low, 0.0)))
+    mine = (lane >= HALF) == (kept_half(member, lax.axis_index("c")) == 1)
+    packet_ref[KEPT - 1] = jnp.where(mine, kept, parts).astype(BF)
 
 
 def prepare_kernel(ctrl_ref, init_ref, target_ref, pieces_ref, begin_ref):
@@ -85,32 +108,49 @@
 
 def chain_kernel(
     amps_ref, meta_ref, own_ref, other_ref, pieces_ref, begin_ref, out_ref,
-    even_h, odd_h, x_ref, base_ref, work_ref,
+    even_h, odd_h, x_ref, base_ref,
 ):
     core = lax.axis_index("c")
     backward = this_member() >= SLOTS // 2
 
-    def lay(block_row, _):
-        base = block_row * BLOCK
+    def piece(block_row, step):
         zl_of = lax.div(block_row, X)
         x_of = lax.rem(block_row, X)
-        for step in range(KEPT):
-            col = lax.rem(block_row + step, NB) * BLOCK
-            mine, theirs = (
-                jnp.concatenate([ref[x_of * Y + y, zl_of * PIECES + step] for y in range(Y)], axis=0)
-                for ref in (own_ref, other_ref)
-            )
-            first = jnp.where(core == 0, mine, theirs)
-            second = jnp.where(core == 0, theirs, mine)
-            block = jnp.concatenate([first, second], axis=0)
-            turned = block.T if 0 < step < NB // 2 else None
-            for ham in (even_h, odd_h):
-                ham[at(base), at(col)] = block
-                if turned is not None:
-                    ham[at(col), at(base)] = turned
+        mine, theirs = (
+            jnp.concatenate([ref[x_of * Y + y, zl_of * KEPT + step] for y in range(Y)], axis=0)
+            for ref in (own_ref, other_ref)
+        )
+        first = jnp.where(core == 0, mine, theirs)
+        second = jnp.where(core == 0, theirs, mine)
+        return jnp.concatenate([first, second], axis=0)
+
+    def put(row, col, block):
+        for ham in (even_h, odd_h):
+            ham[at(row * BLOCK), at(col * BLOCK)] = block
+
+    def lay(block_row, _):
+        put(block_row, block_row, piece(block_row, 0))
+        for step in range(1, KEPT - 1):
+            col = lax.rem(block_row + step, NB)
+            block = piece(block_row, step)
+            put(block_row, col, block)
+            put(col, block_row, block.T)
         return 0
 
     lax.fori_loop(0, NB, lay, 0)
+    low_row = lax.broadcasted_iota(jnp.int32, (BLOCK, BLOCK), 0) < HALF
+    low_col = lax.broadcasted_iota(jnp.int32, (BLOCK, BLOCK), 1) < HALF
+    diagonal = jnp.where(low_row == low_col, 1.0, 0.0).astype(BF)
+    crossed = jnp.where(low_row == low_col, 0.0, 1.0).astype(BF)
+
+    def lay_shared(block_row, _):
+        col = block_row + NB // 2
+        upper, lower = piece(block_row, KEPT - 1), piece(col, KEPT - 1)
+        put(block_row, col, upper * diagonal + lower.T * crossed)
+        put(col, block_row, upper.T * diagonal + lower * crossed)
+        return 0
+
+    lax.fori_loop(0, NB // 2, lay_shared, 0, unroll=2)
 
     def gather_base(p, _):
         base_ref[p] = even_h[at(meta_ref[0, p]), at(meta_ref[1, p])]
@@ -118,24 +158,23 @@
 
     lax.fori_loop(0, 2 * CONTROLS, gather_base, 0)
 
-    def scaled(p, slot):
-        lead = meta_ref[2, p]
-        start = jnp.where(lead == p, base_ref[p].astype(jnp.float32), work_ref[lead])
-        amp = amps_ref[slot, p % CONTROLS]
-        work_ref[lead] = start + amp * pieces_ref[p].astype(jnp.float32)
-
-    def placed(p, target):
-        value = work_ref[meta_ref[2, p]].astype(BF)
-        target[at(meta_ref[0, p]), at(meta_ref[1, p])] = value
-
     def slot_of(step):
         return jnp.where(backward, SLOTS - 1 - step, step)
 
     def tasks(step, target):
         slot = slot_of(jnp.minimum(step, SLOTS - 1))
-        adds = [functools.partial(scaled, p, slot) for p in range(2 * CONTROLS)]
-        puts = [functools.partial(placed, p, target) for p in range(2 * CONTROLS)]
-        return adds + puts
+        total = [None]
+
+        def task(p):
+            which = meta_ref[2, p]
+            start = base_ref[p].astype(jnp.float32)
+            if p > 0:
+                start = jnp.where(meta_ref[3, p] == 0, start, total[0])
+            amp = amps_ref[slot, lax.rem(which, CONTROLS)]
+            total[0] = start + amp * pieces_ref[which].astype(jnp.float32)
+            target[at(meta_ref[0, p]), at(meta_ref[1, p])] = total[0].astype(BF)
+
+        return [functools.partial(task, p) for p in range(2 * CONTROLS)]
 
     x_ref[...] = begin_ref[...]
 
@@ -160,17 +199,17 @@
         found = []
         for n in range(NB // 2):
             found.append(mm(rounded, ham[:, n * 256 : (n + 1) * 256]))
-            for task in todo[2 * n : 2 * n + 2]:
+            for task in todo[n : n + 1]:
                 task()
         return jnp.concatenate(found, axis=1)
 
     def advance(step, ham, following):
         todo = tasks(step + 1, following)
         start = x_ref[...]
-        u1 = applied(start, ham, todo[0:16])
-        u2 = applied(u1, ham, todo[16:32]) * (1.0 / 2)
-        u3 = applied(u2, ham, todo[32:48]) * (1.0 / 3)
-        u4 = applied(u3, ham, todo[48:64]) * (1.0 / 4)
+        u1 = applied(start, ham, todo[0:8])
+        u2 = applied(u1, ham, todo[8:16]) * (1.0 / 2)
+        u3 = applied(u2, ham, todo[16:24]) * (1.0 / 3)
+        u4 = applied(u3, ham, todo[24:32]) * (1.0 / 4)
         x_ref[...] = (start - u2 + u4) + sign * pltpu.roll(u1 - u3, 4, axis=0)
         place = jnp.where(backward, SLOTS - 2 - step, step)
 
@@ -195,6 +234,17 @@
 
 def smem():
     return pl.BlockSpec(memory_space=pltpu.SMEM)
+
+
+def source(drift, amps):
+    return pl.pallas_call(
+        source_kernel,
+        out_shape=jax.ShapeDtypeStruct((KEPT, 4, BLOCK), BF),
+        in_specs=[vmem(), vmem()],
+        out_specs=vmem(),
+        compiler_params=pltpu.CompilerParams(vmem_limit_bytes=2 << 20),
+        name="source",
+    )(drift, jnp.pad(jnp.concatenate([amps] * 2), ((0, 0), (0, HALF - CONTROLS))).reshape(1, BLOCK))
 
 
 def prepare(ctrl_blocks, init_states, targets):
@@ -206,7 +256,7 @@
         ),
         in_specs=[vmem()] * 3,
         out_specs=(vmem(), vmem()),
-        compiler_params=pltpu.CompilerParams(vmem_limit_bytes=16 << 20),
+        compiler_params=pltpu.CompilerParams(vmem_limit_bytes=6 << 20),
         cost_estimate=pl.CostEstimate(
             flops=2 * 3 * CONTROLS * BLOCK**3, bytes_accessed=8 << 20, transcendentals=0
         ),
@@ -226,7 +276,6 @@
             pltpu.VMEM((extent, extent), BF),
             pltpu.VMEM((8, extent), jnp.float32),
             pltpu.VMEM((2 * CONTROLS, BLOCK, BLOCK), BF),
-            pltpu.VMEM((2 * CONTROLS, BLOCK, BLOCK), jnp.float32),
         ],
         compiler_params=pltpu.CompilerParams(vmem_limit_bytes=30 << 20),
         cost_estimate=pl.CostEstimate(
@@ -284,16 +333,9 @@
             pltpu.VMEM((NB, 64, BLOCK), jnp.float32),
             pltpu.VMEM((CONTROLS, BLOCK), jnp.float32),
         ],
-        compiler_params=pltpu.CompilerParams(vmem_limit_bytes=32 << 20),
+        compiler_params=pltpu.CompilerParams(vmem_limit_bytes=8 << 20),
         name="finish",
     )(pos, got, ctrl_blocks)
-
-
-def three_parts(values):
-    high = lax.reduce_precision(values, 8, 7)
-    middle = lax.reduce_precision(values - high, 8, 7)
-    low = lax.reduce_precision(values - high - middle, 8, 7)
-    return jnp.concatenate([high, middle, low, jnp.zeros_like(low)], axis=0).astype(BF)
 
 
 def shared(values, axes, count):
@@ -302,34 +344,32 @@
 
 
 def shards(drift, ctrl_blocks, blk_pos, amps, init_states, targets):
-    member = this_member()
     pieces, begin = prepare(ctrl_blocks, init_states, targets)
-    twice = jnp.concatenate([drift, drift], axis=1)
-    kept = lax.dynamic_slice(twice, (0, member * BLOCK), (4, KEPT * BLOCK))
-    kept = jnp.einsum(
-        "rjl,ml->jrm", kept.reshape(4, KEPT, BLOCK), pick_matrix(BF), preferred_element_type=BF
-    )
-    amps_rows = jnp.pad(three_parts(amps), ((0, 0), (0, BLOCK - CONTROLS)))
-    packet = jnp.concatenate([kept, amps_rows[None]], axis=0)
-    over_z = shared(packet, ("zl", "zh"), ZL * ZH)
-    over_z = over_z.reshape(ZL, ZH, PIECES, 4, BLOCK).transpose(0, 2, 1, 3, 4)
-    own = shared(over_z.reshape(ZL * PIECES, ZH * 4, BLOCK), ("x", "y"), X * Y)
+    over_z = shared(source(drift, amps), ("zl", "zh"), ZL * ZH)
+    over_z = over_z.reshape(ZL, ZH, KEPT, 4, BLOCK).transpose(0, 2, 1, 3, 4)
+    own = shared(over_z.reshape(ZL * KEPT, ZH * 4, BLOCK), ("x", "y"), X * Y)
     other = lax.ppermute(own, "c", [(0, 1), (1, 0)])
-    sent = own.reshape(X, Y, ZL, PIECES, 16, BLOCK)[:, 0, :, KEPT, 0:3, 0:CONTROLS]
-    amps_all = jnp.sum(sent.astype(jnp.float32), axis=2).transpose(1, 0, 2).reshape(SLOTS, CONTROLS)
-
-    first, second = blk_pos[:, 0], blk_pos[:, 1]
-    rows = jnp.concatenate([first, second])
-    cols = jnp.concatenate([second, first])
-    code = rows * NB + cols
-    same = code[:, None] == code[None, :]
-    lead = jnp.min(jnp.where(same, jnp.arange(2 * CONTROLS)[None, :], 2 * CONTROLS), axis=1)
-    meta = jnp.stack([rows * BLOCK, cols * BLOCK, lead]).astype(jnp.int32)
+    sent = own.reshape(X, Y, ZL, KEPT, 16, BLOCK)[:, 0, :, KEPT - 1, 0:3]
+    sent = jnp.sum(sent.astype(jnp.float32), axis=2).transpose(1, 0, 2).reshape(SLOTS, BLOCK)
+    free = 1 - kept_half(jnp.arange(SLOTS)[:, None], lax.axis_index("c"))
+    amps_all = jnp.where(free == 0, sent[:, 0:CONTROLS], sent[:, HALF : HALF + CONTROLS])
+
+    rows = jnp.concatenate([blk_pos[:, 0], blk_pos[:, 1]])
+    cols = jnp.concatenate([blk_pos[:, 1], blk_pos[:, 0]])
+    number = jnp.arange(2 * CONTROLS)
+    key = (rows * NB + cols) * (2 * CONTROLS) + number
+    rank = jnp.sum(key[None, :] < key[:, None], axis=1)
+    chosen = rank[None, :] == number[:, None]
+    key = jnp.sum(jnp.where(chosen, key[None, :], 0), axis=1)
+    place = key // (2 * CONTROLS)
+    again = jnp.concatenate([jnp.zeros((1,), bool), place[1:] == place[:-1]])
+    meta = jnp.stack([place // NB * BLOCK, place % NB * BLOCK, key % (2 * CONTROLS), again])
+    meta = meta.astype(jnp.int32)
 
     out = chain(amps_all, meta, own, other, pieces, begin)
     got = lax.all_to_all(out, ("zl", "x"), 0, 0)
     states, partial_grads = finish(blk_pos, got, ctrl_blocks)
-    grads = lax.psum(lax.psum(partial_grads, ("y", "c")), "zh")
+    grads = jnp.sum(shared(partial_grads, ("y", "zh", "c"), Y * ZH * CORES), axis=0)
     return states[None], grads
 
 

time: 205 us -> 199 us (0.971)
  blocking collectives: 88.5 us -> 83.8 us
  starting transfers between devices: 14.8 us -> 12.4 us
    psum x2 -> x0, blocking collectives: 25.3 us -> none  [shards(): grads = lax.psum(lax.psum(partial_grads, ('y', 'c')), 'zh')]
    all_to_all x2 -> x3, blocking collectives: 63.2 us -> 83.8 us  [shared(): return lax.all_to_all(spread, axes, 0, 0)]
where the time goes in v3:
time: 199 us; the launch traced here: 198 us
  Pallas kernels  87.4 us (44%)
  blocking collectives  83.8 us (42%)
  starting transfers between devices  12.4 us (6%)
  waiting for transfers between devices  10.1 us (5%)
    all_to_all x3, blocking collectives, shared(): return lax.all_to_all(spread, axes, 0, 0)  83.8 us
    pallas_call x1, Pallas kernels, chain(): pl.pallas_call(chain_kernel, out_shape=jax.ShapeDtypeStruct((SLOTS, 64, B...  81.8 us
    all_to_all x1, waiting for transfers between devices, shards(): got = lax.all_to_all(out, ('zl', 'x'), 0, 0)  9.83 us
    ppermute x1, starting transfers between devices, shards(): other = lax.ppermute(own, 'c', [(0, 1), (1, 0)])  6.95 us
    all_to_all x1, starting transfers between devices, shards(): got = lax.all_to_all(out, ('zl', 'x'), 0, 0)  5.49 us
  transfers between devices with their start and end apart: 2, of which 2 were waited for; matrix products, arithmetic and copies ran while one was open for 0% of the time, Pallas kernels for 2%

profile of v3, /device:TPU:1, one launch (start us, length us, event | category | flops | bytes accessed | tf_op | source)
XLA Modules:
  0.0 198.1 jit_solution(15258390225093578821)
XLA Ops:
  0.6 0.7 select_maximum_fusion
  1.4 0.1 reshape.281.amps_ref
  1.5 0.7 copy-done.3
  2.2 0.3 source.1
  2.4 0.1 broadcast_in_dim.59
  2.5 27.9 %all_to_all.20 = bf16[16,9,4,128]{3,2,1,0:T(4,128)(2,1)S(1)} all-to-all(bf16[16,9,4,128]{3,2,1,0:T(4,128)(2,1)S(1)} %broadcast_in_dim.59), channel_id=1, replica_groups=mesh['zl'=4,'x'=4,'y'=4,'zh'=4,'c'=2] {'zl','zh'}, dimensions={0} | all-to-all | bytes 294912 | tf_op jit(solution)/shard_map/all_to_all | solution.py:343
  30.5 0.4 broadcast_in_dim.61
  31.0 33.6 %all_to_all.21.own_ref = bf16[16,36,16,128]{3,2,1,0:T(8,128)(2,1)S(1)} all-to-all(bf16[16,36,16,128]{3,2,1,0:T(8,128)(2,1)S(1)} %broadcast_in_dim.61), channel_id=1, replica_groups=mesh['zl'=4,'x'=4,'y'=4,'zh'=4,'c'=2] {'x','y'}, dimensions={0} | all-to-all | bytes 4718592 | tf_op jit(solution)/shard_map/all_to_all | solution.py:343
  64.5 7.0 %collective-permute-start = (bf16[16,36,16,128]{3,2,1,0:T(8,128)(2,1)S(1)}, bf16[16,36,16,128]{3,2,1,0:T(8,128)(2,1)}, u32[]{:S(2)}, u32[]{:S(2)}) collective-permute-start(bf16[16,36,16,128]{3,2,1,0:T(8,128)(2,1)S(1)} %all_to_all.21.own_ref), channel_id=1, source_target_pairs={{0,1},{1,0},{2,3},{3,2},{4,5},{5,4},{6,7},{7,6},{8,9},{9,8},{10,11... | collective-permute-start | bytes 7077896 | tf_op jit(solution)/shard_map/ppermute | solution.py:351
  71.5 3.2 %prepare.1 = (bf16[32,128,128]{2,1,0:T(8,128)(2,1)S(1)}, f32[8,2048]{1,0:T(8,128)S(1)}) custom-call(bf16[16,128,128]{2,1,0:T(8,128)(2,1)S(1)} %copy-done, f32[2,16,2048]{2,1,0:T(8,128)S(1)} %copy-done.1, f32[2,16,2048]{2,1,0:T(8,128)S(1)} %copy-done.2), custom_call_target="tpu_custom_call" | custom-call | flops 201326592 | bytes 8388608 | tf_op jit(solution)/shard_map/prepare/pallas_call | solution.py:251
  74.8 0.1 iota_add_fusion
  74.9 0.2 convert_reduce_fusion.1
  75.1 0.1 select_reduce_fusion
  75.2 0.1 compare_bitcast_fusion
  75.3 0.1 add_convert_fusion
  75.5 0.1 slice_select_fusion.amps_ref
  75.5 0.2 collective-permute-done.other_ref
  75.8 81.8 %chain.1 = bf16[16,64,128]{2,1,0:T(8,128)(2,1)} custom-call(f32[16,16]{1,0:T(8,128)S(1)} %slice_select_fusion.amps_ref, s32[4,32]{1,0:T(4,128)S(1)} %pad_add_fusion.meta_ref, bf16[16,36,16,128]{3,2,1,0:T(8,128)(2,1)S(1)} %all_to_all.21.own_ref, bf16[16,36,16,128]{3,2,1,0:T(8,128)(2,1)} %collective-permute-done.other_ref, ...), custom_call_target="tpu_custom_call" | custom-call | flops 4294967296 | bytes 8388608 | tf_op jit(solution)/shard_map/chain/pallas_call | solution.py:269
  157.6 5.5 %all-to-all-start.2 = ((bf16[16,64,128]{2,1,0:T(8,128)(2,1)}), bf16[16,64,128]{2,1,0:T(8,128)(2,1)S(1)}, u32[]{:S(2)}, u32[]{:S(2)}) async-start(bf16[16,64,128]{2,1,0:T(8,128)(2,1)} %chain.1), calls=%async_computation.2 | async-start | bytes 524288 | tf_op jit(solution)/shard_map/all_to_all | solution.py:370
  163.1 0.1 copy.23.pos_ref
  163.2 9.8 %all-to-all-done.2.got_ref = bf16[16,64,128]{2,1,0:T(8,128)(2,1)S(1)} async-done(((bf16[16,64,128]{2,1,0:T(8,128)(2,1)}), bf16[16,64,128]{2,1,0:T(8,128)(2,1)S(1)}, u32[]{:S(2)}, u32[]{:S(2)}) %all-to-all-start.2) | async-done | bytes 262176 | tf_op jit(solution)/shard_map/all_to_all | solution.py:370
  173.0 2.1 %finish.1 = (f32[2,16,2048]{2,1,0:T(8,128)}, f32[1,16]{1,0:T(1,128)S(1)}) custom-call(s32[16,2]{1,0:T(8,128)S(1)} %copy.23.pos_ref, bf16[16,64,128]{2,1,0:T(8,128)(2,1)S(1)} %all-to-all-done.2.got_ref, bf16[16,128,128]{2,1,0:T(8,128)(2,1)S(1)} %copy-done), custom_call_target="tpu_custom_call" | custom-call | tf_op jit(solution)/shard_map/finish/pallas_call | solution.py:322
  175.1 22.4 %all_to_all.22 = f32[32,1,16]{2,1,0:T(1,128)S(1)} all-to-all(f32[32,1,16]{2,1,0:T(1,128)S(1)} %broadcast_in_dim.65), channel_id=1, replica_groups=mesh['zl'=4,'x'=4,'y'=4,'zh'=4,'c'=2] {'y','zh','c'}, dimensions={0} | all-to-all | bytes 4096 | tf_op jit(solution)/shard_map/all_to_all | solution.py:343
  197.5 0.6 reduce_sum.44
  (19 shorter events, 0.2 us)
Async XLA Ops:
  1.5 0.7 copy-start.3
  30.9 40.6 %copy-start = (bf16[16,128,128]{2,1,0:T(8,128)(2,1)S(1)}, bf16[16,128,128]{2,1,0:T(8,128)(2,1)}, u32[]{:S(2)}) copy-start(bf16[16,128,128]{2,1,0:T(8,128)(2,1)} %ctrl_ref.3) | copy-start | bytes 1572868
  30.9 40.6 %copy-start.1 = (f32[2,16,2048]{2,1,0:T(8,128)S(1)}, f32[2,16,2048]{2,1,0:T(8,128)}, u32[]{:S(2)}) copy-start(f32[2,16,2048]{2,1,0:T(8,128)} %init_ref.1) | copy-start | bytes 786436
  31.0 40.6 %copy-start.2 = (f32[2,16,2048]{2,1,0:T(8,128)S(1)}, f32[2,16,2048]{2,1,0:T(8,128)}, u32[]{:S(2)}) copy-start(f32[2,16,2048]{2,1,0:T(8,128)} %target_ref.1) | copy-start | bytes 786436
  31.0 43.8 %copy-start.4 = (s32[16,2]{0,1:T(2,128)S(1)}, s32[16,2]{0,1:T(2,128)}, u32[]{:S(2)}) copy-start(s32[16,2]{0,1:T(2,128)} %param.8) | copy-start | bytes 388
  64.5 11.2 %collective-permute-start = (bf16[16,36,16,128]{3,2,1,0:T(8,128)(2,1)S(1)}, bf16[16,36,16,128]{3,2,1,0:T(8,128)(2,1)}, u32[]{:S(2)}, u32[]{:S(2)}) collective-permute-start(bf16[16,36,16,128]{3,2,1,0:T(8,128)(2,1)S(1)} %all_to_all.21.own_ref), channel_id=1, source_target_pairs={{0,1},{1,0},{2,3},{3,2},{4,5},{5,4},{6,7},{7,6},{8,9},{9,8},{10,11... | collective-permute-start | bytes 7077896 | tf_op jit(solution)/shard_map/ppermute | solution.py:351
  157.6 15.4 %all-to-all-start.2 = ((bf16[16,64,128]{2,1,0:T(8,128)(2,1)}), bf16[16,64,128]{2,1,0:T(8,128)(2,1)S(1)}, u32[]{:S(2)}, u32[]{:S(2)}) async-start(bf16[16,64,128]{2,1,0:T(8,128)(2,1)} %chain.1), calls=%async_computation.2 | async-start | bytes 524288 | tf_op jit(solution)/shard_map/all_to_all | solution.py:370

commit v4 on v3

--- a/solution.py
+++ b/solution.py
@@ -59,13 +59,17 @@
         packet_ref[step] = mm_t(drift_ref[:, at(block * BLOCK)], pick).astype(BF)
     block = lax.rem(member + KEPT - 1, NB)
     kept = mm_t(drift_ref[:, at(block * BLOCK)], pick)
-    row = lax.broadcasted_iota(jnp.int32, (4, BLOCK), 0)
     lane = lax.broadcasted_iota(jnp.int32, (4, BLOCK), 1)
     amps = amps_ref[...]
     high = amps.astype(BF).astype(jnp.float32)
     middle = (amps - high).astype(BF).astype(jnp.float32)
     low = amps - high - middle
-    parts = jnp.where(row == 0, high, jnp.where(row == 1, middle, jnp.where(row == 2, low, 0.0)))
+    part = lax.broadcasted_iota(jnp.int32, (4, CONTROLS), 0)
+    parts = jnp.where(part == 0, high, jnp.where(part == 1, middle, jnp.where(part == 2, low, 0.0)))
+    number = lax.broadcasted_iota(jnp.int32, (CONTROLS, BLOCK), 0)
+    column = lax.broadcasted_iota(jnp.int32, (CONTROLS, BLOCK), 1)
+    spread = jnp.where((column & (HALF - 1)) == number, 1.0, 0.0).astype(BF)
+    parts = mm(parts.astype(BF), spread)
     mine = (lane >= HALF) == (kept_half(member, lax.axis_index("c")) == 1)
     packet_ref[KEPT - 1] = jnp.where(mine, kept, parts).astype(BF)
 
@@ -107,8 +111,8 @@
 
 
 def chain_kernel(
-    amps_ref, meta_ref, own_ref, other_ref, pieces_ref, begin_ref, out_ref,
-    even_h, odd_h, x_ref, base_ref,
+    amps_ref, meta_ref, own_ref, sent_ref, pieces_ref, begin_ref, out_ref,
+    even_h, odd_h, x_ref, base_ref, other_ref, sems,
 ):
     core = lax.axis_index("c")
     backward = this_member() >= SLOTS // 2
@@ -128,16 +132,29 @@
         for ham in (even_h, odd_h):
             ham[at(row * BLOCK), at(col * BLOCK)] = block
 
-    def lay(block_row, _):
+    def lay(block_row):
         put(block_row, block_row, piece(block_row, 0))
         for step in range(1, KEPT - 1):
             col = lax.rem(block_row + step, NB)
             block = piece(block_row, step)
             put(block_row, col, block)
             put(col, block_row, block.T)
-        return 0
-
-    lax.fori_loop(0, NB, lay, 0)
+
+    def fetch(x_of):
+        part = pl.ds(x_of * Y, Y)
+        return pltpu.make_async_copy(sent_ref.at[part], other_ref.at[part], sems.at[x_of])
+
+    for x_of in range(X):
+        fetch(x_of).start()
+    for x_of in range(X):
+        fetch(x_of).wait()
+
+        def lay_next(zl_of, _, x_of=x_of):
+            lay(zl_of * X + x_of)
+            return 0
+
+        lax.fori_loop(0, ZL, lay_next, 0)
+
     low_row = lax.broadcasted_iota(jnp.int32, (BLOCK, BLOCK), 0) < HALF
     low_col = lax.broadcasted_iota(jnp.int32, (BLOCK, BLOCK), 1) < HALF
     diagonal = jnp.where(low_row == low_col, 1.0, 0.0).astype(BF)
@@ -244,7 +261,7 @@
         out_specs=vmem(),
         compiler_params=pltpu.CompilerParams(vmem_limit_bytes=2 << 20),
         name="source",
-    )(drift, jnp.pad(jnp.concatenate([amps] * 2), ((0, 0), (0, HALF - CONTROLS))).reshape(1, BLOCK))
+    )(drift, amps)
 
 
 def prepare(ctrl_blocks, init_states, targets):
@@ -269,13 +286,15 @@
     return pl.pallas_call(
         chain_kernel,
         out_shape=jax.ShapeDtypeStruct((SLOTS, 64, BLOCK), BF),
-        in_specs=[smem(), smem()] + [vmem()] * 4,
+        in_specs=[smem(), smem(), vmem(), pl.BlockSpec(memory_space=pl.ANY), vmem(), vmem()],
         out_specs=vmem(),
         scratch_shapes=[
             pltpu.VMEM((extent, extent), BF),
             pltpu.VMEM((extent, extent), BF),
             pltpu.VMEM((8, extent), jnp.float32),
             pltpu.VMEM((2 * CONTROLS, BLOCK, BLOCK), BF),
+            pltpu.VMEM((X * Y, ZL * KEPT, 16, BLOCK), BF),
+            pltpu.SemaphoreType.DMA((X,)),
         ],
         compiler_params=pltpu.CompilerParams(vmem_limit_bytes=30 << 20),
         cost_estimate=pl.CostEstimate(

time: 199 us -> 199 us (level)
  no operation moved by 1% of the time
where the time goes in v4:
time: 199 us; the launch traced here: 198 us
  Pallas kernels  87.8 us (44%)
  blocking collectives  83.8 us (42%)
  starting transfers between devices  12.5 us (6%)
  waiting for transfers between devices  10.1 us (5%)
  local copies, waits for them, and re-layouts  2.12 us (1%)
    all_to_all x3, blocking collectives, shared(): return lax.all_to_all(spread, axes, 0, 0)  83.8 us
    pallas_call x1, Pallas kernels, chain(): pl.pallas_call(chain_kernel, out_shape=jax.ShapeDtypeStruct((SLOTS, 64, B...  82.1 us
    all_to_all x1, waiting for transfers between devices, shards(): got = lax.all_to_all(out, ('zl', 'x'), 0, 0)  9.83 us
    ppermute x1, starting transfers between devices, shards(): other = lax.ppermute(own, 'c', [(0, 1), (1, 0)])  6.95 us
    all_to_all x1, starting transfers between devices, shards(): got = lax.all_to_all(out, ('zl', 'x'), 0, 0)  5.5 us
  transfers between devices with their start and end apart: 2, of which 2 were waited for; matrix products, arithmetic and copies ran while one was open for 0% of the time, Pallas kernels for 2%

profile of v4, /device:TPU:1, one launch (start us, length us, event | category | flops | bytes accessed | tf_op | source)
XLA Modules:
  0.0 198.2 jit_solution(626451103230338020)
XLA Ops:
  0.6 0.7 copy-done.3
  1.4 0.7 copy-done.4
  2.0 0.3 source.1
  2.3 0.1 broadcast_in_dim.59
  2.3 27.9 %all_to_all.20 = bf16[16,9,4,128]{3,2,1,0:T(4,128)(2,1)S(1)} all-to-all(bf16[16,9,4,128]{3,2,1,0:T(4,128)(2,1)S(1)} %broadcast_in_dim.59), channel_id=1, replica_groups=mesh['zl'=4,'x'=4,'y'=4,'zh'=4,'c'=2] {'zl','zh'}, dimensions={0} | all-to-all | bytes 294912 | tf_op jit(solution)/shard_map/all_to_all | solution.py:362
  30.2 0.1 copy.21
  30.3 0.4 broadcast_in_dim.61
  30.8 33.6 %all_to_all.21.own_ref = bf16[16,36,16,128]{3,2,1,0:T(8,128)(2,1)S(1)} all-to-all(bf16[16,36,16,128]{3,2,1,0:T(8,128)(2,1)S(1)} %broadcast_in_dim.61), channel_id=1, replica_groups=mesh['zl'=4,'x'=4,'y'=4,'zh'=4,'c'=2] {'x','y'}, dimensions={0} | all-to-all | bytes 4718592 | tf_op jit(solution)/shard_map/all_to_all | solution.py:362
  64.4 7.0 %collective-permute-start = (bf16[16,36,16,128]{3,2,1,0:T(8,128)(2,1)S(1)}, bf16[16,36,16,128]{3,2,1,0:T(8,128)(2,1)}, u32[]{:S(2)}, u32[]{:S(2)}) collective-permute-start(bf16[16,36,16,128]{3,2,1,0:T(8,128)(2,1)S(1)} %all_to_all.21.own_ref), channel_id=1, source_target_pairs={{0,1},{1,0},{2,3},{3,2},{4,5},{5,4},{6,7},{7,6},{8,9},{9,8},{10,11... | collective-permute-start | bytes 7077896 | tf_op jit(solution)/shard_map/ppermute | solution.py:370
  71.4 3.2 %prepare.1 = (bf16[32,128,128]{2,1,0:T(8,128)(2,1)S(1)}, f32[8,2048]{1,0:T(8,128)S(1)}) custom-call(bf16[16,128,128]{2,1,0:T(8,128)(2,1)S(1)} %copy-done, f32[2,16,2048]{2,1,0:T(8,128)S(1)} %copy-done.1, f32[2,16,2048]{2,1,0:T(8,128)S(1)} %copy-done.2), custom_call_target="tpu_custom_call" | custom-call | flops 201326592 | bytes 8388608 | tf_op jit(solution)/shard_map/prepare/pallas_call | solution.py:268
  74.7 0.1 iota_add_fusion
  74.7 0.2 convert_reduce_fusion.1
  74.9 0.1 select_reduce_fusion
  75.1 0.1 compare_bitcast_fusion
  75.1 0.1 add_convert_fusion
  75.3 0.1 slice_select_fusion.amps_ref
  75.4 0.2 collective-permute-done.sent_ref
  75.6 82.1 %chain.1 = bf16[16,64,128]{2,1,0:T(8,128)(2,1)} custom-call(f32[16,16]{1,0:T(8,128)S(1)} %slice_select_fusion.amps_ref, s32[4,32]{1,0:T(4,128)S(1)} %pad_add_fusion.meta_ref, bf16[16,36,16,128]{3,2,1,0:T(8,128)(2,1)S(1)} %all_to_all.21.own_ref, bf16[16,36,16,128]{3,2,1,0:T(8,128)(2,1)} %collective-permute-done.sent_ref, ...), custom_call_target="tpu_custom_call" | custom-call | flops 4294967296 | bytes 8388608 | tf_op jit(solution)/shard_map/chain/pallas_call | solution.py:286
  157.7 5.5 %all-to-all-start.2 = ((bf16[16,64,128]{2,1,0:T(8,128)(2,1)}), bf16[16,64,128]{2,1,0:T(8,128)(2,1)S(1)}, u32[]{:S(2)}, u32[]{:S(2)}) async-start(bf16[16,64,128]{2,1,0:T(8,128)(2,1)} %chain.1), calls=%async_computation.2 | async-start | bytes 524288 | tf_op jit(solution)/shard_map/all_to_all | solution.py:389
  163.3 0.1 copy.23.pos_ref
  163.3 9.8 %all-to-all-done.2.got_ref = bf16[16,64,128]{2,1,0:T(8,128)(2,1)S(1)} async-done(((bf16[16,64,128]{2,1,0:T(8,128)(2,1)}), bf16[16,64,128]{2,1,0:T(8,128)(2,1)S(1)}, u32[]{:S(2)}, u32[]{:S(2)}) %all-to-all-start.2) | async-done | bytes 262176 | tf_op jit(solution)/shard_map/all_to_all | solution.py:389
  173.2 2.1 %finish.1 = (f32[2,16,2048]{2,1,0:T(8,128)}, f32[1,16]{1,0:T(1,128)S(1)}) custom-call(s32[16,2]{1,0:T(8,128)S(1)} %copy.23.pos_ref, bf16[16,64,128]{2,1,0:T(8,128)(2,1)S(1)} %all-to-all-done.2.got_ref, bf16[16,128,128]{2,1,0:T(8,128)(2,1)S(1)} %copy-done), custom_call_target="tpu_custom_call" | custom-call | tf_op jit(solution)/shard_map/finish/pallas_call | solution.py:341
  175.3 22.4 %all_to_all.22 = f32[32,1,16]{2,1,0:T(1,128)S(1)} all-to-all(f32[32,1,16]{2,1,0:T(1,128)S(1)} %broadcast_in_dim.65), channel_id=1, replica_groups=mesh['zl'=4,'x'=4,'y'=4,'zh'=4,'c'=2] {'y','zh','c'}, dimensions={0} | all-to-all | bytes 4096 | tf_op jit(solution)/shard_map/all_to_all | solution.py:362
  197.7 0.6 reduce_sum.44
  (19 shorter events, 0.2 us)
Async XLA Ops:
  0.6 0.7 copy-start.3
  1.3 0.7 copy-start.4
  30.8 40.6 %copy-start = (bf16[16,128,128]{2,1,0:T(8,128)(2,1)S(1)}, bf16[16,128,128]{2,1,0:T(8,128)(2,1)}, u32[]{:S(2)}) copy-start(bf16[16,128,128]{2,1,0:T(8,128)(2,1)} %ctrl_ref.3) | copy-start | bytes 1572868
  30.8 40.6 %copy-start.1 = (f32[2,16,2048]{2,1,0:T(8,128)S(1)}, f32[2,16,2048]{2,1,0:T(8,128)}, u32[]{:S(2)}) copy-start(f32[2,16,2048]{2,1,0:T(8,128)} %init_ref.1) | copy-start | bytes 786436
  30.8 40.6 %copy-start.2 = (f32[2,16,2048]{2,1,0:T(8,128)S(1)}, f32[2,16,2048]{2,1,0:T(8,128)}, u32[]{:S(2)}) copy-start(f32[2,16,2048]{2,1,0:T(8,128)} %target_ref.1) | copy-start | bytes 786436
  30.8 43.8 %copy-start.5 = (s32[16,2]{0,1:T(2,128)S(1)}, s32[16,2]{0,1:T(2,128)}, u32[]{:S(2)}) copy-start(s32[16,2]{0,1:T(2,128)} %param.8) | copy-start | bytes 388
  64.4 11.2 %collective-permute-start = (bf16[16,36,16,128]{3,2,1,0:T(8,128)(2,1)S(1)}, bf16[16,36,16,128]{3,2,1,0:T(8,128)(2,1)}, u32[]{:S(2)}, u32[]{:S(2)}) collective-permute-start(bf16[16,36,16,128]{3,2,1,0:T(8,128)(2,1)S(1)} %all_to_all.21.own_ref), channel_id=1, source_target_pairs={{0,1},{1,0},{2,3},{3,2},{4,5},{5,4},{6,7},{7,6},{8,9},{9,8},{10,11... | collective-permute-start | bytes 7077896 | tf_op jit(solution)/shard_map/ppermute | solution.py:370
  157.7 15.4 %all-to-all-start.2 = ((bf16[16,64,128]{2,1,0:T(8,128)(2,1)}), bf16[16,64,128]{2,1,0:T(8,128)(2,1)S(1)}, u32[]{:S(2)}, u32[]{:S(2)}) async-start(bf16[16,64,128]{2,1,0:T(8,128)(2,1)} %chain.1), calls=%async_computation.2 | async-start | bytes 524288 | tf_op jit(solution)/shard_map/all_to_all | solution.py:389

commit v5 on v4

--- a/solution.py
+++ b/solution.py
@@ -12,6 +12,7 @@
 NB = 16
 KEPT = NB // 2 + 1
 HALF = BLOCK // 2
+BAND = 64
 SLOTS = 16
 CONTROLS = 16
 BF = jnp.bfloat16
@@ -182,16 +183,19 @@
         slot = slot_of(jnp.minimum(step, SLOTS - 1))
         total = [None]
 
-        def task(p):
+        def task(q):
+            band, p = divmod(q, 2 * CONTROLS)
+            part = slice(band * BAND, (band + 1) * BAND)
             which = meta_ref[2, p]
-            start = base_ref[p].astype(jnp.float32)
+            start = base_ref[p, part].astype(jnp.float32)
             if p > 0:
                 start = jnp.where(meta_ref[3, p] == 0, start, total[0])
             amp = amps_ref[slot, lax.rem(which, CONTROLS)]
-            total[0] = start + amp * pieces_ref[which].astype(jnp.float32)
-            target[at(meta_ref[0, p]), at(meta_ref[1, p])] = total[0].astype(BF)
-
-        return [functools.partial(task, p) for p in range(2 * CONTROLS)]
+            total[0] = start + amp * pieces_ref[which, part].astype(jnp.float32)
+            rows = pl.ds(pl.multiple_of(meta_ref[0, p] + band * BAND, BAND), BAND)
+            target[rows, at(meta_ref[1, p])] = total[0].astype(BF)
+
+        return [functools.partial(task, q) for q in range(2 * CONTROLS * BLOCK // BAND)]
 
     x_ref[...] = begin_ref[...]
 
@@ -208,26 +212,29 @@
     def _():
         write(SLOTS - 1)
 
-    row_of = lax.broadcasted_iota(jnp.int32, (8, NB * BLOCK), 0)
+    row_of = lax.broadcasted_iota(jnp.int32, (8, BLOCK), 0)
     sign = jnp.where((row_of < 4) == jnp.logical_not(backward), 1.0, -1.0)
+    sign = jnp.concatenate([sign] * NB, axis=1)
 
     def applied(values, ham, todo):
         rounded = values.astype(BF)
         found = []
         for n in range(NB // 2):
             found.append(mm(rounded, ham[:, n * 256 : (n + 1) * 256]))
-            for task in todo[n : n + 1]:
+            for task in todo[2 * n : 2 * n + 2]:
                 task()
         return jnp.concatenate(found, axis=1)
 
     def advance(step, ham, following):
         todo = tasks(step + 1, following)
         start = x_ref[...]
-        u1 = applied(start, ham, todo[0:8])
-        u2 = applied(u1, ham, todo[8:16]) * (1.0 / 2)
-        u3 = applied(u2, ham, todo[16:24]) * (1.0 / 3)
-        u4 = applied(u3, ham, todo[24:32]) * (1.0 / 4)
-        x_ref[...] = (start - u2 + u4) + sign * pltpu.roll(u1 - u3, 4, axis=0)
+        u1 = applied(start, ham, todo[0:16])
+        x_ref[...] = sign * pltpu.roll(u1, 4, axis=0) + start
+        u2 = applied(u1, ham, todo[16:32]) * (1.0 / 2)
+        u3 = applied(u2, ham, todo[32:48]) * (1.0 / 3)
+        x_ref[...] = x_ref[...] - u2 - sign * pltpu.roll(u3, 4, axis=0)
+        u4 = applied(u3, ham, todo[48:64]) * (1.0 / 4)
+        x_ref[...] = x_ref[...] + u4
         place = jnp.where(backward, SLOTS - 2 - step, step)
 
         @pl.when(place >= 0)

time: 199 us -> 197 us (0.990)
  no operation moved by 1% of the time
where the time goes in v5:
time: 197 us; the launch traced here: 196 us
  Pallas kernels  85.9 us (44%)
  blocking collectives  83.8 us (43%)
  starting transfers between devices  12.5 us (6%)
  waiting for transfers between devices  10.1 us (5%)
  local copies, waits for them, and re-layouts  2.12 us (1%)
    all_to_all x3, blocking collectives, shared(): return lax.all_to_all(spread, axes, 0, 0)  83.8 us
    pallas_call x1, Pallas kernels, chain(): pl.pallas_call(chain_kernel, out_shape=jax.ShapeDtypeStruct((SLOTS, 64, B...  80.3 us
    all_to_all x1, waiting for transfers between devices, shards(): got = lax.all_to_all(out, ('zl', 'x'), 0, 0)  9.83 us
    ppermute x1, starting transfers between devices, shards(): other = lax.ppermute(own, 'c', [(0, 1), (1, 0)])  6.95 us
    all_to_all x1, starting transfers between devices, shards(): got = lax.all_to_all(out, ('zl', 'x'), 0, 0)  5.5 us
  transfers between devices with their start and end apart: 2, of which 2 were waited for; matrix products, arithmetic and copies ran while one was open for 0% of the time, Pallas kernels for 2%

profile of v5, /device:TPU:1, one launch (start us, length us, event | category | flops | bytes accessed | tf_op | source)
XLA Modules:
  0.0 196.4 jit_solution(18181410150348377987)
XLA Ops:
  0.6 0.7 copy-done.3
  1.4 0.7 copy-done.4
  2.0 0.3 source.1
  2.3 0.1 broadcast_in_dim.59
  2.3 27.9 %all_to_all.20 = bf16[16,9,4,128]{3,2,1,0:T(4,128)(2,1)S(1)} all-to-all(bf16[16,9,4,128]{3,2,1,0:T(4,128)(2,1)S(1)} %broadcast_in_dim.59), channel_id=1, replica_groups=mesh['zl'=4,'x'=4,'y'=4,'zh'=4,'c'=2] {'zl','zh'}, dimensions={0} | all-to-all | bytes 294912 | tf_op jit(solution)/shard_map/all_to_all | solution.py:369
  30.2 0.1 copy.21
  30.3 0.4 broadcast_in_dim.61
  30.8 33.6 %all_to_all.21.own_ref = bf16[16,36,16,128]{3,2,1,0:T(8,128)(2,1)S(1)} all-to-all(bf16[16,36,16,128]{3,2,1,0:T(8,128)(2,1)S(1)} %broadcast_in_dim.61), channel_id=1, replica_groups=mesh['zl'=4,'x'=4,'y'=4,'zh'=4,'c'=2] {'x','y'}, dimensions={0} | all-to-all | bytes 4718592 | tf_op jit(solution)/shard_map/all_to_all | solution.py:369
  64.4 7.0 %collective-permute-start = (bf16[16,36,16,128]{3,2,1,0:T(8,128)(2,1)S(1)}, bf16[16,36,16,128]{3,2,1,0:T(8,128)(2,1)}, u32[]{:S(2)}, u32[]{:S(2)}) collective-permute-start(bf16[16,36,16,128]{3,2,1,0:T(8,128)(2,1)S(1)} %all_to_all.21.own_ref), channel_id=1, source_target_pairs={{0,1},{1,0},{2,3},{3,2},{4,5},{5,4},{6,7},{7,6},{8,9},{9,8},{10,11... | collective-permute-start | bytes 7077896 | tf_op jit(solution)/shard_map/ppermute | solution.py:377
  71.4 3.2 %prepare.1 = (bf16[32,128,128]{2,1,0:T(8,128)(2,1)S(1)}, f32[8,2048]{1,0:T(8,128)S(1)}) custom-call(bf16[16,128,128]{2,1,0:T(8,128)(2,1)S(1)} %copy-done, f32[2,16,2048]{2,1,0:T(8,128)S(1)} %copy-done.1, f32[2,16,2048]{2,1,0:T(8,128)S(1)} %copy-done.2), custom_call_target="tpu_custom_call" | custom-call | flops 201326592 | bytes 8388608 | tf_op jit(solution)/shard_map/prepare/pallas_call | solution.py:275
  74.7 0.1 iota_add_fusion
  74.7 0.2 convert_reduce_fusion.1
  74.9 0.1 select_reduce_fusion
  75.1 0.1 compare_bitcast_fusion
  75.1 0.1 add_convert_fusion
  75.3 0.1 slice_select_fusion.amps_ref
  75.4 0.2 collective-permute-done.sent_ref
  75.6 80.3 %chain.1 = bf16[16,64,128]{2,1,0:T(8,128)(2,1)} custom-call(f32[16,16]{1,0:T(8,128)S(1)} %slice_select_fusion.amps_ref, s32[4,32]{1,0:T(4,128)S(1)} %pad_add_fusion.meta_ref, bf16[16,36,16,128]{3,2,1,0:T(8,128)(2,1)S(1)} %all_to_all.21.own_ref, bf16[16,36,16,128]{3,2,1,0:T(8,128)(2,1)} %collective-permute-done.sent_ref, ...), custom_call_target="tpu_custom_call" | custom-call | flops 4294967296 | bytes 8388608 | tf_op jit(solution)/shard_map/chain/pallas_call | solution.py:293
  155.9 5.5 %all-to-all-start.2 = ((bf16[16,64,128]{2,1,0:T(8,128)(2,1)}), bf16[16,64,128]{2,1,0:T(8,128)(2,1)S(1)}, u32[]{:S(2)}, u32[]{:S(2)}) async-start(bf16[16,64,128]{2,1,0:T(8,128)(2,1)} %chain.1), calls=%async_computation.2 | async-start | bytes 524288 | tf_op jit(solution)/shard_map/all_to_all | solution.py:396
  161.4 0.1 copy.23.pos_ref
  161.5 9.8 %all-to-all-done.2.got_ref = bf16[16,64,128]{2,1,0:T(8,128)(2,1)S(1)} async-done(((bf16[16,64,128]{2,1,0:T(8,128)(2,1)}), bf16[16,64,128]{2,1,0:T(8,128)(2,1)S(1)}, u32[]{:S(2)}, u32[]{:S(2)}) %all-to-all-start.2) | async-done | bytes 262176 | tf_op jit(solution)/shard_map/all_to_all | solution.py:396
  171.3 2.1 %finish.1 = (f32[2,16,2048]{2,1,0:T(8,128)}, f32[1,16]{1,0:T(1,128)S(1)}) custom-call(s32[16,2]{1,0:T(8,128)S(1)} %copy.23.pos_ref, bf16[16,64,128]{2,1,0:T(8,128)(2,1)S(1)} %all-to-all-done.2.got_ref, bf16[16,128,128]{2,1,0:T(8,128)(2,1)S(1)} %copy-done), custom_call_target="tpu_custom_call" | custom-call | tf_op jit(solution)/shard_map/finish/pallas_call | solution.py:348
  173.4 22.4 %all_to_all.22 = f32[32,1,16]{2,1,0:T(1,128)S(1)} all-to-all(f32[32,1,16]{2,1,0:T(1,128)S(1)} %broadcast_in_dim.65), channel_id=1, replica_groups=mesh['zl'=4,'x'=4,'y'=4,'zh'=4,'c'=2] {'y','zh','c'}, dimensions={0} | all-to-all | bytes 4096 | tf_op jit(solution)/shard_map/all_to_all | solution.py:369
  195.8 0.6 reduce_sum.44
  (19 shorter events, 0.2 us)
Async XLA Ops:
  0.6 0.7 copy-start.3
  1.3 0.7 copy-start.4
  30.8 40.6 %copy-start = (bf16[16,128,128]{2,1,0:T(8,128)(2,1)S(1)}, bf16[16,128,128]{2,1,0:T(8,128)(2,1)}, u32[]{:S(2)}) copy-start(bf16[16,128,128]{2,1,0:T(8,128)(2,1)} %ctrl_ref.3) | copy-start | bytes 1572868
  30.8 40.6 %copy-start.1 = (f32[2,16,2048]{2,1,0:T(8,128)S(1)}, f32[2,16,2048]{2,1,0:T(8,128)}, u32[]{:S(2)}) copy-start(f32[2,16,2048]{2,1,0:T(8,128)} %init_ref.1) | copy-start | bytes 786436
  30.8 40.6 %copy-start.2 = (f32[2,16,2048]{2,1,0:T(8,128)S(1)}, f32[2,16,2048]{2,1,0:T(8,128)}, u32[]{:S(2)}) copy-start(f32[2,16,2048]{2,1,0:T(8,128)} %target_ref.1) | copy-start | bytes 786436
  30.8 43.8 %copy-start.5 = (s32[16,2]{0,1:T(2,128)S(1)}, s32[16,2]{0,1:T(2,128)}, u32[]{:S(2)}) copy-start(s32[16,2]{0,1:T(2,128)} %param.8) | copy-start | bytes 388
  64.4 11.2 %collective-permute-start = (bf16[16,36,16,128]{3,2,1,0:T(8,128)(2,1)S(1)}, bf16[16,36,16,128]{3,2,1,0:T(8,128)(2,1)}, u32[]{:S(2)}, u32[]{:S(2)}) collective-permute-start(bf16[16,36,16,128]{3,2,1,0:T(8,128)(2,1)S(1)} %all_to_all.21.own_ref), channel_id=1, source_target_pairs={{0,1},{1,0},{2,3},{3,2},{4,5},{5,4},{6,7},{7,6},{8,9},{9,8},{10,11... | collective-permute-start | bytes 7077896 | tf_op jit(solution)/shard_map/ppermute | solution.py:377
  155.9 15.4 %all-to-all-start.2 = ((bf16[16,64,128]{2,1,0:T(8,128)(2,1)}), bf16[16,64,128]{2,1,0:T(8,128)(2,1)S(1)}, u32[]{:S(2)}, u32[]{:S(2)}) async-start(bf16[16,64,128]{2,1,0:T(8,128)(2,1)} %chain.1), calls=%async_computation.2 | async-start | bytes 524288 | tf_op jit(solution)/shard_map/all_to_all | solution.py:396

commit v6 on v5

--- a/solution.py
+++ b/solution.py
@@ -154,7 +154,7 @@
             lay(zl_of * X + x_of)
             return 0
 
-        lax.fori_loop(0, ZL, lay_next, 0)
+        lax.fori_loop(0, ZL, lay_next, 0, unroll=2)
 
     low_row = lax.broadcasted_iota(jnp.int32, (BLOCK, BLOCK), 0) < HALF
     low_col = lax.broadcasted_iota(jnp.int32, (BLOCK, BLOCK), 1) < HALF

time: 197 us -> 197 us (level)
  no operation moved by 1% of the time
where the time goes in v6:
time: 197 us; the launch traced here: 196 us
  Pallas kernels  85.6 us (43%)
  blocking collectives  83.8 us (43%)
  starting transfers between devices  12.5 us (6%)
  waiting for transfers between devices  10.1 us (5%)
  local copies, waits for them, and re-layouts  2.12 us (1%)
    all_to_all x3, blocking collectives, shared(): return lax.all_to_all(spread, axes, 0, 0)  83.8 us
    pallas_call x1, Pallas kernels, chain(): pl.pallas_call(chain_kernel, out_shape=jax.ShapeDtypeStruct((SLOTS, 64, B...  80 us
    all_to_all x1, waiting for transfers between devices, shards(): got = lax.all_to_all(out, ('zl', 'x'), 0, 0)  9.83 us
    ppermute x1, starting transfers between devices, shards(): other = lax.ppermute(own, 'c', [(0, 1), (1, 0)])  6.95 us
    all_to_all x1, starting transfers between devices, shards(): got = lax.all_to_all(out, ('zl', 'x'), 0, 0)  5.5 us
  transfers between devices with their start and end apart: 2, of which 2 were waited for; matrix products, arithmetic and copies ran while one was open for 0% of the time, Pallas kernels for 2%

profile of v6, /device:TPU:1, one launch (start us, length us, event | category | flops | bytes accessed | tf_op | source)
XLA Modules:
  0.0 196.1 jit_solution(10772355049974787761)
XLA Ops:
  0.6 0.7 copy-done.3
  1.4 0.7 copy-done.4
  2.0 0.3 source.1
  2.3 0.1 broadcast_in_dim.59
  2.3 27.9 %all_to_all.20 = bf16[16,9,4,128]{3,2,1,0:T(4,128)(2,1)S(1)} all-to-all(bf16[16,9,4,128]{3,2,1,0:T(4,128)(2,1)S(1)} %broadcast_in_dim.59), channel_id=1, replica_groups=mesh['zl'=4,'x'=4,'y'=4,'zh'=4,'c'=2] {'zl','zh'}, dimensions={0} | all-to-all | bytes 294912 | tf_op jit(solution)/shard_map/all_to_all | solution.py:369
  30.2 0.1 copy.21
  30.3 0.4 broadcast_in_dim.61
  30.8 33.6 %all_to_all.21.own_ref = bf16[16,36,16,128]{3,2,1,0:T(8,128)(2,1)S(1)} all-to-all(bf16[16,36,16,128]{3,2,1,0:T(8,128)(2,1)S(1)} %broadcast_in_dim.61), channel_id=1, replica_groups=mesh['zl'=4,'x'=4,'y'=4,'zh'=4,'c'=2] {'x','y'}, dimensions={0} | all-to-all | bytes 4718592 | tf_op jit(solution)/shard_map/all_to_all | solution.py:369
  64.4 7.0 %collective-permute-start = (bf16[16,36,16,128]{3,2,1,0:T(8,128)(2,1)S(1)}, bf16[16,36,16,128]{3,2,1,0:T(8,128)(2,1)}, u32[]{:S(2)}, u32[]{:S(2)}) collective-permute-start(bf16[16,36,16,128]{3,2,1,0:T(8,128)(2,1)S(1)} %all_to_all.21.own_ref), channel_id=1, source_target_pairs={{0,1},{1,0},{2,3},{3,2},{4,5},{5,4},{6,7},{7,6},{8,9},{9,8},{10,11... | collective-permute-start | bytes 7077896 | tf_op jit(solution)/shard_map/ppermute | solution.py:377
  71.4 3.2 %prepare.1 = (bf16[32,128,128]{2,1,0:T(8,128)(2,1)S(1)}, f32[8,2048]{1,0:T(8,128)S(1)}) custom-call(bf16[16,128,128]{2,1,0:T(8,128)(2,1)S(1)} %copy-done, f32[2,16,2048]{2,1,0:T(8,128)S(1)} %copy-done.1, f32[2,16,2048]{2,1,0:T(8,128)S(1)} %copy-done.2), custom_call_target="tpu_custom_call" | custom-call | flops 201326592 | bytes 8388608 | tf_op jit(solution)/shard_map/prepare/pallas_call | solution.py:275
  74.7 0.1 iota_add_fusion
  74.7 0.2 convert_reduce_fusion.1
  74.9 0.1 select_reduce_fusion
  75.1 0.1 compare_bitcast_fusion
  75.1 0.1 add_convert_fusion
  75.3 0.1 slice_select_fusion.amps_ref
  75.4 0.2 collective-permute-done.sent_ref
  75.6 80.0 %chain.1 = bf16[16,64,128]{2,1,0:T(8,128)(2,1)} custom-call(f32[16,16]{1,0:T(8,128)S(1)} %slice_select_fusion.amps_ref, s32[4,32]{1,0:T(4,128)S(1)} %pad_add_fusion.meta_ref, bf16[16,36,16,128]{3,2,1,0:T(8,128)(2,1)S(1)} %all_to_all.21.own_ref, bf16[16,36,16,128]{3,2,1,0:T(8,128)(2,1)} %collective-permute-done.sent_ref, ...), custom_call_target="tpu_custom_call" | custom-call | flops 4294967296 | bytes 8388608 | tf_op jit(solution)/shard_map/chain/pallas_call | solution.py:293
  155.6 5.5 %all-to-all-start.2 = ((bf16[16,64,128]{2,1,0:T(8,128)(2,1)}), bf16[16,64,128]{2,1,0:T(8,128)(2,1)S(1)}, u32[]{:S(2)}, u32[]{:S(2)}) async-start(bf16[16,64,128]{2,1,0:T(8,128)(2,1)} %chain.1), calls=%async_computation.2 | async-start | bytes 524288 | tf_op jit(solution)/shard_map/all_to_all | solution.py:396
  161.1 0.1 copy.23.pos_ref
  161.2 9.8 %all-to-all-done.2.got_ref = bf16[16,64,128]{2,1,0:T(8,128)(2,1)S(1)} async-done(((bf16[16,64,128]{2,1,0:T(8,128)(2,1)}), bf16[16,64,128]{2,1,0:T(8,128)(2,1)S(1)}, u32[]{:S(2)}, u32[]{:S(2)}) %all-to-all-start.2) | async-done | bytes 262176 | tf_op jit(solution)/shard_map/all_to_all | solution.py:396
  171.0 2.1 %finish.1 = (f32[2,16,2048]{2,1,0:T(8,128)}, f32[1,16]{1,0:T(1,128)S(1)}) custom-call(s32[16,2]{1,0:T(8,128)S(1)} %copy.23.pos_ref, bf16[16,64,128]{2,1,0:T(8,128)(2,1)S(1)} %all-to-all-done.2.got_ref, bf16[16,128,128]{2,1,0:T(8,128)(2,1)S(1)} %copy-done), custom_call_target="tpu_custom_call" | custom-call | tf_op jit(solution)/shard_map/finish/pallas_call | solution.py:348
  173.1 22.4 %all_to_all.22 = f32[32,1,16]{2,1,0:T(1,128)S(1)} all-to-all(f32[32,1,16]{2,1,0:T(1,128)S(1)} %broadcast_in_dim.65), channel_id=1, replica_groups=mesh['zl'=4,'x'=4,'y'=4,'zh'=4,'c'=2] {'y','zh','c'}, dimensions={0} | all-to-all | bytes 4096 | tf_op jit(solution)/shard_map/all_to_all | solution.py:369
  195.5 0.6 reduce_sum.44
  (19 shorter events, 0.2 us)
Async XLA Ops:
  0.6 0.7 copy-start.3
  1.3 0.7 copy-start.4
  30.8 40.6 %copy-start = (bf16[16,128,128]{2,1,0:T(8,128)(2,1)S(1)}, bf16[16,128,128]{2,1,0:T(8,128)(2,1)}, u32[]{:S(2)}) copy-start(bf16[16,128,128]{2,1,0:T(8,128)(2,1)} %ctrl_ref.3) | copy-start | bytes 1572868
  30.8 40.6 %copy-start.1 = (f32[2,16,2048]{2,1,0:T(8,128)S(1)}, f32[2,16,2048]{2,1,0:T(8,128)}, u32[]{:S(2)}) copy-start(f32[2,16,2048]{2,1,0:T(8,128)} %init_ref.1) | copy-start | bytes 786436
  30.8 40.6 %copy-start.2 = (f32[2,16,2048]{2,1,0:T(8,128)S(1)}, f32[2,16,2048]{2,1,0:T(8,128)}, u32[]{:S(2)}) copy-start(f32[2,16,2048]{2,1,0:T(8,128)} %target_ref.1) | copy-start | bytes 786436
  30.8 43.8 %copy-start.5 = (s32[16,2]{0,1:T(2,128)S(1)}, s32[16,2]{0,1:T(2,128)}, u32[]{:S(2)}) copy-start(s32[16,2]{0,1:T(2,128)} %param.8) | copy-start | bytes 388
  64.4 11.2 %collective-permute-start = (bf16[16,36,16,128]{3,2,1,0:T(8,128)(2,1)S(1)}, bf16[16,36,16,128]{3,2,1,0:T(8,128)(2,1)}, u32[]{:S(2)}, u32[]{:S(2)}) collective-permute-start(bf16[16,36,16,128]{3,2,1,0:T(8,128)(2,1)S(1)} %all_to_all.21.own_ref), channel_id=1, source_target_pairs={{0,1},{1,0},{2,3},{3,2},{4,5},{5,4},{6,7},{7,6},{8,9},{9,8},{10,11... | collective-permute-start | bytes 7077896 | tf_op jit(solution)/shard_map/ppermute | solution.py:377
  155.6 15.4 %all-to-all-start.2 = ((bf16[16,64,128]{2,1,0:T(8,128)(2,1)}), bf16[16,64,128]{2,1,0:T(8,128)(2,1)S(1)}, u32[]{:S(2)}, u32[]{:S(2)}) async-start(bf16[16,64,128]{2,1,0:T(8,128)(2,1)} %chain.1), calls=%async_computation.2 | async-start | bytes 524288 | tf_op jit(solution)/shard_map/all_to_all | solution.py:396
